TPU v7x, 32 devices: a whole 2x2x4 slice. The times are simulated.
32 devices in a mesh: dp: 4 (over y, x), tensor: 8 (over z, core).
Axes of the slice: x: 2, y: 2, z: 4, core: 2. Of those that a mesh axis runs over, the one named last changes fastest.
Arguments:
- hidden_act: bfloat16 [2816, 36864], P('dp', 'tensor'), may hold values from -80 to 80
- out_grad: bfloat16 [2816, 4608], P('dp', 'tensor'), may hold values from -0.5 to 0.5
- other_sq: float32 [8], P('dp'), may hold values from 2989699 to 597939968
Outputs:
- weight_grad: float32 [4608, 36864], P('dp', 'tensor')
All inputs are finite; a program needn't handle non-finite values.
Results may differ from a plain program's by a relative error of at most 0.002.
Values may be sent and summed in bfloat16 or wider, within the bound.
No kernel may reach another device: no remote copies, remote signals or barrier semaphores. Data moves between devices by JAX's collectives and lax.ppermute only.
A program may use at most 128 MiB of HBM per device.

v0:
```python
import functools
import math

import jax
import jax.numpy as jnp
from jax import lax
from jax.experimental import pallas as pl
from jax.experimental.pallas import tpu as pltpu
from jax.sharding import PartitionSpec as P


BF16, F32 = jnp.bfloat16, jnp.float32
CLIP_DIVISOR = 80.0
VMEM_LIMIT = 57 << 20
NEAR_SHARES = (2, 3, 2, 2)
CHUNK_SHARES = (2, 3, 2, 1, 1)


def bits_of(mask):
    return [1 << i for i in range(mask.bit_length()) if mask >> i & 1]


def swap(x, axis, size, mask):
    return lax.ppermute(x, axis, [(i, i ^ mask) for i in range(size)])


def after(*arrays):
    return lax.optimization_barrier(arrays)


def cut(total, shares):
    if total % (2 * sum(shares)):
        shares = (1,)
    unit, start, pieces = total // sum(shares), 0, []
    for share in shares:
        pieces.append((start, share * unit))
        start += share * unit
    return pieces


def row_block(rows):
    for block in (288, 192, 144, 128, 96, 64, 48, 32, 16, 8):
        if rows % block == 0:
            return block
    return rows


def matmul_kernel(terms, block, tiles, adds, *refs):
    grad_ref, out_ref, refs = refs[0], refs[-1], refs[1:]

    def multiply(side):
        for at in range(0, out_ref.shape[0], block):
            here = pl.ds(at, block)
            total, k = (refs[-2][here, :] if adds else None), 0
            for s, arrays in terms:
                act_ref = refs[k + side % arrays]
                k += arrays
                product = jnp.dot(grad_ref[s, here, :], act_ref[...], preferred_element_type=F32)
                total = product if total is None else total + product
            out_ref[here, :] = total

    if any(arrays > 1 for _, arrays in terms):
        step = pl.program_id(0)
        pl.when(step < tiles)(lambda: multiply(0))
        pl.when(step >= tiles)(lambda: multiply(1))
    else:
        multiply(0)


def chunk_matmul(grads, acts, out, start, width, adds, out_shape):
    _, rows, tokens = grads.shape
    tile = math.gcd(width // 2, 256)
    tiles = width // 2 // tile
    specs, args, terms = [pl.BlockSpec(memory_space=pltpu.VMEM)], [grads], []
    args = [pltpu.with_memory_space_constraint(grads, pltpu.VMEM)]
    for s, (array, other) in acts.items():
        if isinstance(other, int):
            maps = [(array, lambda j, at=other // tile: (0, at + j))]
        else:
            maps = [
                (array, lambda j: (0, jnp.minimum(j, tiles - 1))),
                (other, lambda j: (0, jnp.maximum(j - tiles, 0))),
            ]
        for array, index in maps:
            args.append(array)
            specs.append(pl.BlockSpec((tokens, tile), index))
        terms.append((s, len(maps)))
    window = pl.BlockSpec((rows, tile), lambda j: (0, start // tile + j))
    aliases = {}
    if out is not None:
        specs.append(window if adds else pl.BlockSpec(memory_space=pl.ANY))
        args.append(out)
        aliases = {len(args) - 1: 0}
    return pl.pallas_call(
        functools.partial(matmul_kernel, terms, row_block(rows), tiles, adds),
        grid=(2 * tiles,),
        in_specs=specs,
        out_specs=window,
        out_shape=jax.ShapeDtypeStruct(out_shape, F32),
        input_output_aliases=aliases,
        compiler_params=pltpu.CompilerParams(vmem_limit_bytes=VMEM_LIMIT),
        cost_estimate=pl.CostEstimate(
            flops=2 * rows * width * len(terms) * tokens,
            bytes_accessed=2 * len(terms) * tokens * width + 4 * rows * width * (1 + adds),
            transcendentals=0,
        ),
        name="chunk_matmul",
    )(*args)


def prepare_kernel(n, where_ref, scale_ref, *refs):
    pieces, out_ref = refs[:n], refs[n]
    step = pl.program_id(0)
    scale = scale_ref[...]
    for k in range(n):

        @pl.when(step == k)
        def _(k=k):
            piece = pieces[k][...]
            out_ref[...] = (piece.astype(F32) * scale[:, None, None, :]).astype(BF16)[:, :, None]


def prepare(pieces, where, scale):
    n = len(pieces)
    groups, halves, rows, tokens = pieces[0].shape
    whole = pl.BlockSpec((groups, halves, rows, tokens), lambda k, w: (0, 0, 0, 0))
    return pl.pallas_call(
        functools.partial(prepare_kernel, n),
        grid_spec=pltpu.PrefetchScalarGridSpec(
            num_scalar_prefetch=1,
            grid=(n,),
            in_specs=[pl.BlockSpec((groups, tokens), lambda k, w: (0, 0))] + [whole] * n,
            out_specs=pl.BlockSpec(
                (groups, halves, 1, rows, tokens), lambda k, w: (0, 0, w[k], 0, 0)
            ),
        ),
        out_shape=jax.ShapeDtypeStruct((groups, halves, n, rows, tokens), BF16),
        cost_estimate=pl.CostEstimate(
            flops=groups * halves * n * rows * tokens,
            bytes_accessed=4 * groups * halves * n * rows * tokens,
            transcendentals=0,
        ),
        compiler_params=pltpu.CompilerParams(vmem_limit_bytes=VMEM_LIMIT),
        name="prepare",
    )(where, scale, *pieces)


def on_device(n_dp, n_tensor, hidden_act, out_grad, other_sq):
    examples = other_sq.shape[0]
    tokens, columns = hidden_act.shape
    features = out_grad.shape[1]
    length = tokens // examples
    chips = n_tensor // 2
    me = lax.axis_index("dp")
    place = lax.axis_index("tensor")

    near = [1 << i for i in range(n_dp.bit_length() - 1)]
    spans = cut(columns, NEAR_SHARES)
    parts, held = [], hidden_act
    for start, width in spans:
        parts.append(lax.slice_in_dim(held, start, start + width, axis=1))
        held = after(held, parts[-1])[0]
    blocks = {mask: [swap(parts[0], "dp", n_dp, mask)] for mask in near}

    grad = out_grad.T
    share = features // n_tensor
    spread = lax.all_to_all(grad.reshape(n_tensor, share, tokens), "tensor", split_axis=0, concat_axis=0, tiled=True)
    halves = n_tensor // n_dp
    spread = spread.reshape(n_dp, halves, share, tokens)
    mine = [
        lax.dynamic_index_in_dim(spread, me ^ s, 0, keepdims=False) for s in range(n_dp)
    ]
    exchanged = [swap(mine[s], "dp", n_dp, s) for s in range(1, n_dp)]
    for p in range(1, len(spans)):
        for mask in near:
            blocks[mask].append(swap(parts[p], "dp", n_dp, mask))
    piece = jnp.stack([mine[0]] + exchanged)

    acts = hidden_act.reshape(examples, length, columns)
    act_gram = jnp.einsum("etf,esf->ets", acts, acts, preferred_element_type=F32)
    grads = grad.reshape(features, examples, length)
    grad_gram = jnp.einsum("fet,fes->ets", grads, grads, preferred_element_type=F32)
    grams = jnp.stack([act_gram.reshape(tokens, length), grad_gram.reshape(tokens, length)])
    rows, first = tokens, 0
    mask = 1
    while mask < n_tensor:
        rows //= 2
        bit = (place // mask) % 2
        sent = lax.dynamic_slice_in_dim(grams, (1 - bit) * rows, rows, 1)
        kept = lax.dynamic_slice_in_dim(grams, bit * rows, rows, 1)
        grams = kept + swap(sent, "tensor", n_tensor, mask)
        first = first + bit * rows
        mask *= 2
    row_sum = jnp.sum(grams[0] * grams[1], axis=1)
    example = (first + jnp.arange(rows, dtype=jnp.int32)) // length
    layer_sq = jnp.sum(
        jnp.where(example[None] == jnp.arange(examples, dtype=jnp.int32)[:, None], row_sum[None], 0.0),
        axis=1,
    )
    mask = 1
    while mask < n_tensor:
        layer_sq = layer_sq + swap(layer_sq, "tensor", n_tensor, mask)
        mask *= 2
    total_columns, total_features = columns * n_tensor, features * n_tensor
    clip_bound = math.sqrt(length * total_columns * total_features / CLIP_DIVISOR)
    clip_scale = jnp.minimum(1.0, clip_bound / jnp.sqrt(other_sq + layer_sq))
    ring = [(i, (i + 2) % n_tensor) for i in range(n_tensor)]
    piece, clip_scale = after(piece, clip_scale)
    pieces, where = [], []
    for k in range(chips):
        if k:
            piece = lax.ppermute(piece, "tensor", ring)
        origin = (place // 2 - k) % chips * 2
        pieces += [piece, swap(piece, "tensor", n_tensor, 1)]
        where += [origin + place % 2, origin + (place + 1) % 2]
    scales = jnp.stack([clip_scale] + [swap(clip_scale, "dp", n_dp, s) for s in range(1, n_dp)])
    token_scale = jnp.broadcast_to(scales[:, :, None], (n_dp, examples, length)).reshape(n_dp, tokens)
    scaled = prepare(pieces, jnp.stack(where).astype(jnp.int32), token_scale)
    scaled = scaled.reshape(n_dp, halves * n_tensor * share, tokens)

    def own_or_near(start):
        p = max(i for i, (first, _) in enumerate(spans) if first <= start)
        return {0: (hidden_act, start), **{m: (blocks[m][p], start - spans[p][0]) for m in near}}

    chunks = cut(columns, CHUNK_SHARES)
    out_shape = (scaled.shape[1], columns)
    ahead = [c for c, (start, _) in enumerate(chunks) if start >= spans[-1][0]] if len(spans) > 1 else []
    ahead = ahead if n_dp > 2 else []
    out = None
    if ahead:
        first = chunks[ahead[0]][0]
        out = chunk_matmul(scaled, own_or_near(first), out, first, columns - first, False, out_shape)
    for c, (start, width) in enumerate(chunks):
        half = width // 2
        known = own_or_near(start)
        halves_of = {}
        for side in (0, 1):
            for mask, (array, at) in known.items():
                halves_of[mask, side] = (array, at + side * half)
        far = sorted((m for m in range(n_dp) if m not in known), key=lambda m: len(bits_of(m)))
        acts = {}
        for mask in far:
            bits = bits_of(mask)
            for side in (0, 1):
                bit = bits[(2 * c + side) % len(bits)]
                source, at = halves_of[mask ^ bit, side]
                if source.shape[1] != half:
                    source = lax.slice_in_dim(source, at, at + half, axis=1)
                halves_of[mask, side] = (swap(source, "dp", n_dp, bit), 0)
            acts[mask] = (halves_of[mask, 0][0], halves_of[mask, 1][0])
        if c not in ahead:
            acts = {**known, **acts}
        out = chunk_matmul(scaled, acts, out, start, width, c in ahead, out_shape)
    return out


def solution(mesh):
    placed = (P("dp", "tensor"), P("dp", "tensor"), P("dp"))

    def body(hidden_act, out_grad, other_sq):
        return on_device(
            mesh.shape["dp"], mesh.shape["tensor"], hidden_act, out_grad, other_sq
        )

    return jax.shard_map(
        body, mesh=mesh, in_specs=placed, out_specs=P("dp", "tensor"), check_vma=False
    )
```

profile of v0, /device:TPU:0, one launch (start us, length us, event | category | flops | bytes accessed | tf_op | source)
XLA Modules:
  0.0 312.5 jit_solution(12840660496353562831)
XLA Ops:
  0.0 2.6 reshape.36
  3.4 9.6 %fusion.9 = f32[2,352,352]{2,1,0:T(8,128)} fusion(bf16[2,352,4608]{2,1,0:T(8,128)(2,1)} %bitcast.37), kind=kOutput, calls=%fused_computation.27 | convolution fusion | flops 2283798528 | bytes 7479296 | tf_op jit(solution)/shard_map/etf,esf->ets/dot_general | solution.py:180
  15.7 6.0 %all-to-all-start = ((bf16[8,72,704]{2,1,0:T(8,128)(2,1)}), bf16[8,72,704]{2,1,0:T(8,128)(2,1)}, u32[]{:S(2)}, u32[]{:S(2)}) async-start(bf16[8,72,704]{2,1,0:T(8,128)(2,1)} %bitcast.45), calls=%async_computation | async-start | bytes 1769472 | tf_op jit(solution)/shard_map/all_to_all | solution.py:167
  26.4 2.6 slice.50
  34.6 10.3 %all-to-all-done = bf16[8,72,704]{2,1,0:T(8,128)(2,1)} async-done(((bf16[8,72,704]{2,1,0:T(8,128)(2,1)}), bf16[8,72,704]{2,1,0:T(8,128)(2,1)}, u32[]{:S(2)}, u32[]{:S(2)}) %all-to-all-start) | async-done | bytes 811040 | tf_op jit(solution)/shard_map/all_to_all | solution.py:167
  52.0 2.5 collective-permute-start.5
  57.1 19.0 %collective-permute-done.1 = bf16[2,72,704]{2,1,0:T(8,128)(2,1)S(1)} collective-permute-done((bf16[2,72,704]{2,1,0:T(8,128)(2,1)}, bf16[2,72,704]{2,1,0:T(8,128)(2,1)S(1)}, u32[]{:S(2)}, u32[]{:S(2)}) %collective-permute-start.1) | collective-permute-done | bytes 202784 | tf_op jit(solution)/shard_map/ppermute | solution.py:24
  81.2 3.2 %collective-permute-done.7 = f32[2]{0:T(128)S(1)} collective-permute-done((f32[2]{0:T(128)S(1)}, f32[2]{0:T(128)S(1)}, u32[]{:S(2)}, u32[]{:S(2)}) %collective-permute-start.7) | collective-permute-done | bytes 40 | tf_op jit(solution)/shard_map/ppermute | solution.py:24
  84.4 2.4 collective-permute-start.8
  92.8 18.0 %collective-permute-done.34.refs_3_ = bf16[704,1024]{1,0:T(8,128)(2,1)S(1)} collective-permute-done((bf16[704,1024]{1,0:T(8,128)(2,1)}, bf16[704,1024]{1,0:T(8,128)(2,1)S(1)}, u32[]{:S(2)}, u32[]{:S(2)}) %collective-permute-start.34) | collective-permute-done | bytes 1441824 | tf_op jit(solution)/shard_map/ppermute | solution.py:24
  112.7 9.5 %collective-permute-done.33.refs_2_ = bf16[704,1024]{1,0:T(8,128)(2,1)S(1)} collective-permute-done((bf16[704,1024]{1,0:T(8,128)(2,1)}, bf16[704,1024]{1,0:T(8,128)(2,1)S(1)}, u32[]{:S(2)}, u32[]{:S(2)}) %collective-permute-start.33) | collective-permute-done | bytes 1441824 | tf_op jit(solution)/shard_map/ppermute | solution.py:24
  123.7 8.4 %collective-permute-done.15.refs_4_ = bf16[4,2,72,704]{3,2,1,0:T(8,128)(2,1)} collective-permute-done((bf16[4,2,72,704]{3,2,1,0:T(8,128)(2,1)}, bf16[4,2,72,704]{3,2,1,0:T(8,128)(2,1)}, u32[]{:S(2)}, u32[]{:S(2)}) %collective-permute-start.15) | collective-permute-done | bytes 811040 | tf_op jit(solution)/shard_map/ppermute | solution.py:212
  132.5 53.5 %collective-permute-done.26.refs_3_ = bf16[704,1024]{1,0:T(8,128)(2,1)S(1)} collective-permute-done((bf16[704,1024]{1,0:T(8,128)(2,1)}, bf16[704,1024]{1,0:T(8,128)(2,1)S(1)}, u32[]{:S(2)}, u32[]{:S(2)}) %collective-permute-start.26) | collective-permute-done | bytes 1441824 | tf_op jit(solution)/shard_map/ppermute | solution.py:24
  186.0 11.9 %collective-permute-done.25.refs_2_ = bf16[704,1024]{1,0:T(8,128)(2,1)S(1)} collective-permute-done((bf16[704,1024]{1,0:T(8,128)(2,1)}, bf16[704,1024]{1,0:T(8,128)(2,1)S(1)}, u32[]{:S(2)}, u32[]{:S(2)}) %collective-permute-start.25) | collective-permute-done | bytes 1441824 | tf_op jit(solution)/shard_map/ppermute | solution.py:24
  205.1 2.4 collective-permute-start.11
  228.6 8.5 %prepare.1 = bf16[4,2,8,72,704]{4,3,2,1,0:T(8,128)(2,1)} custom-call(s32[8]{0:T(128)} %stack.66.where_ref, f32[4,704]{1,0:T(4,128)} %reshape.37.scale_ref, bf16[4,2,72,704]{3,2,1,0:T(8,128)(2,1)} %copy-done.3, bf16[4,2,72,704]{3,2,1,0:T(8,128)(2,1)} %collective-permute-done.12.refs_1_, bf16[4,2,72,704]{3,2,1,0:T(8,128)(2,1)} %collective-permute-done.13.refs_2_, ...), custom_call_target="tpu_custom_call" | custom-call | flops 3244032 | bytes 12976128 | tf_op jit(solution)/shard_map/prepare/pallas_call | solution.py:127
  237.2 3.0 copy-done
  240.2 8.5 %chunk_matmul.6.refs_6_ = f32[1152,4608]{1,0:T(8,128)} custom-call(bf16[4,1152,704]{2,1,0:T(8,128)(2,1)S(1)} %bitcast.31, bf16[704,4608]{1,0:T(8,128)(2,1)} %refs_1_.7, bf16[704,1024]{1,0:T(8,128)(2,1)} %copy-done.4, bf16[704,1024]{1,0:T(8,128)(2,1)} %collective-permute-done.19.refs_3_), custom_call_target="tpu_custom_call" | custom-call | flops 4982833152 | bytes 9043968 | tf_op jit(solution)/shard_map/chunk_matmul/pallas_call | solution.py:94
  250.8 10.6 %chunk_matmul.7.refs_6_ = f32[1152,4608]{1,0:T(8,128)} custom-call(bf16[4,1152,704]{2,1,0:T(8,128)(2,1)S(1)} %bitcast.32, bf16[704,4608]{1,0:T(8,128)(2,1)} %refs_1_.7, bf16[704,1024]{1,0:T(8,128)(2,1)} %copy-done.7, bf16[704,1024]{1,0:T(8,128)(2,1)} %copy-done.6, bf16[704,512]{1,0:T(8,128)(2,1)} %collective-permute-done.35.refs_4_, ...), custom_call_target="tpu_custom_call", output_to_operand_aliasing={{}: (6, {})} | custom-call | flops 6643777536 | bytes 10485760 | tf_op jit(solution)/shard_map/chunk_matmul/pallas_call | solution.py:94
  261.3 14.7 %collective-permute-done.31.refs_4_ = bf16[704,768]{1,0:T(8,128)(2,1)} collective-permute-done((bf16[704,768]{1,0:T(8,128)(2,1)}, bf16[704,768]{1,0:T(8,128)(2,1)}, u32[]{:S(2)}, u32[]{:S(2)}) %collective-permute-start.31) | collective-permute-done | bytes 1081376 | tf_op jit(solution)/shard_map/ppermute | solution.py:24
  279.0 14.7 %chunk_matmul.8.refs_6_ = f32[1152,4608]{1,0:T(8,128)} custom-call(bf16[4,1152,704]{2,1,0:T(8,128)(2,1)S(1)} %bitcast.33, bf16[704,4608]{1,0:T(8,128)(2,1)} %refs_1_.7, bf16[704,1536]{1,0:T(8,128)(2,1)} %collective-permute-done.29.refs_2_, bf16[704,1536]{1,0:T(8,128)(2,1)} %copy-done.1, ...), custom_call_target="tpu_custom_call", output_to_operand_aliasing={{}: (6, {})} | custom-call | flops 9965666304 | bytes 15728640 | tf_op jit(solution)/shard_map/chunk_matmul/pallas_call | solution.py:94
  294.2 10.6 %chunk_matmul.9.refs_3_ = f32[1152,4608]{1,0:T(8,128)} custom-call(bf16[4,1152,704]{2,1,0:T(8,128)(2,1)S(1)} %bitcast.34, bf16[704,4608]{1,0:T(8,128)(2,1)} %refs_1_.7, bf16[704,1024]{1,0:T(8,128)(2,1)} %copy-done.11, bf16[704,1024]{1,0:T(8,128)(2,1)} %copy-done.9, bf16[704,512]{1,0:T(8,128)(2,1)} %collective-permute-done.27.refs_4_, ...), custom_call_target="tpu_custom_call", output_to_operand_aliasing={{}: (6, {})} | custom-call | flops 6643777536 | bytes 10485760 | tf_op jit(solution)/shard_map/chunk_matmul/pallas_call | solution.py:94
  304.8 3.8 %chunk_matmul.10.refs_3_ = f32[1152,4608]{1,0:T(8,128)} custom-call(bf16[4,1152,704]{2,1,0:T(8,128)(2,1)S(1)} %bitcast.35, bf16[704,256]{1,0:T(8,128)(2,1)} %collective-permute-done.23.refs_1_, bf16[704,256]{1,0:T(8,128)(2,1)} %collective-permute-done.24.refs_2_, f32[1152,4608]{1,0:T(8,128)} %chunk_matmul.9.refs_3_), custom_call_target="tpu_custom_call", output_to_operand_aliasing={{}: (3, {})} | custom-call | flops 830472192 | bytes 5439488 | tf_op jit(solution)/shard_map/chunk_matmul/pallas_call | solution.py:94
  308.7 3.8 %chunk_matmul.11 = f32[1152,4608]{1,0:T(8,128)} custom-call(bf16[4,1152,704]{2,1,0:T(8,128)(2,1)S(1)} %bitcast.36, bf16[704,256]{1,0:T(8,128)(2,1)} %collective-permute-done.20.refs_1_, bf16[704,256]{1,0:T(8,128)(2,1)} %collective-permute-done.22.refs_2_, f32[1152,4608]{1,0:T(8,128)} %chunk_matmul.10.refs_3_), custom_call_target="tpu_custom_call", output_to_operand_aliasing={{}: (3, {})} | custom-call | flops 830472192 | bytes 5439488 | tf_op jit(solution)/shard_map/chunk_matmul/pallas_call | solution.py:94
  (125 shorter events, 72.1 us)
Async XLA Ops:
  15.7 29.2 %all-to-all-start = ((bf16[8,72,704]{2,1,0:T(8,128)(2,1)}), bf16[8,72,704]{2,1,0:T(8,128)(2,1)}, u32[]{:S(2)}, u32[]{:S(2)}) async-start(bf16[8,72,704]{2,1,0:T(8,128)(2,1)} %bitcast.45), calls=%async_computation | async-start | bytes 1769472 | tf_op jit(solution)/shard_map/all_to_all | solution.py:167
  24.4 26.4 %collective-permute-start.4 = (f32[2,176,352]{2,1,0:T(8,128)}, f32[2,176,352]{2,1,0:T(8,128)}, u32[]{:S(2)}, u32[]{:S(2)}) collective-permute-start(f32[2,176,352]{2,1,0:T(8,128)} %constant_dynamic-slice_fusion.1), channel_id=1, source_target_pairs={{0,2},{1,3},{2,0},{3,1},{4,6},{5,7},{6,4},{7,5},{8,10},{9,11},{10,... | collective-permute-start | bytes 1486856 | tf_op jit(solution)/shard_map/ppermute | solution.py:24
  33.1 56.2 %collective-permute-start.19 = (bf16[704,1024]{1,0:T(8,128)(2,1)}, bf16[704,1024]{1,0:T(8,128)(2,1)}, u32[]{:S(2)}, u32[]{:S(2)}) collective-permute-start(bf16[704,1024]{1,0:T(8,128)(2,1)} %slice.53), channel_id=1, source_target_pairs={{0,16},{8,24},{16,0},{24,8},{1,17},{9,25},{17,1},{25,9},{2,18},{10... | collective-permute-start | bytes 4325384 | tf_op jit(solution)/shard_map/ppermute | solution.py:24
  48.6 27.5 %collective-permute-start.1 = (bf16[2,72,704]{2,1,0:T(8,128)(2,1)}, bf16[2,72,704]{2,1,0:T(8,128)(2,1)S(1)}, u32[]{:S(2)}, u32[]{:S(2)}) collective-permute-start(bf16[2,72,704]{2,1,0:T(8,128)(2,1)} %get-tuple-element.21), channel_id=1, source_target_pairs={{0,16},{8,24},{16,0},{24,8},{1,17},{9,25},{17,1},{25,9},{2,18},{10... | collective-permute-start | bytes 608264 | tf_op jit(solution)/shard_map/ppermute | solution.py:24
  50.1 27.5 %collective-permute-start.2 = (bf16[2,72,704]{2,1,0:T(8,128)(2,1)S(1)}, bf16[2,72,704]{2,1,0:T(8,128)(2,1)S(1)}, u32[]{:S(2)}, u32[]{:S(2)}) collective-permute-start(bf16[2,72,704]{2,1,0:T(8,128)(2,1)S(1)} %get-tuple-element.20), channel_id=1, source_target_pairs={{0,24},{8,16},{16,8},{24,0},{1,25},{9,17},{17,9},{25,1},{2,26},{10... | collective-permute-start | bytes 608264 | tf_op jit(solution)/shard_map/ppermute | solution.py:24
  52.0 27.3 %collective-permute-start.5 = (f32[2,88,352]{2,1,0:T(8,128)S(1)}, f32[2,88,352]{2,1,0:T(8,128)S(1)}, u32[]{:S(2)}, u32[]{:S(2)}) collective-permute-start(f32[2,88,352]{2,1,0:T(8,128)S(1)} %constant_dynamic-slice_fusion), channel_id=1, source_target_pairs={{0,4},{1,5},{2,6},{3,7},{4,0},{5,1},{6,2},{7,3},{8,12},{9,13},{10,... | collective-permute-start | bytes 743432 | tf_op jit(solution)/shard_map/ppermute | solution.py:24
  55.6 35.7 %collective-permute-start.21 = (bf16[704,1024]{1,0:T(8,128)(2,1)}, bf16[704,1024]{1,0:T(8,128)(2,1)S(1)}, u32[]{:S(2)}, u32[]{:S(2)}) collective-permute-start(bf16[704,1024]{1,0:T(8,128)(2,1)} %slice.53), channel_id=1, source_target_pairs={{0,8},{8,0},{16,24},{24,16},{1,9},{9,1},{17,25},{25,17},{2,10},{10... | collective-permute-start | bytes 4325384 | tf_op jit(solution)/shard_map/ppermute | solution.py:24
  76.1 34.7 %collective-permute-start.34 = (bf16[704,1024]{1,0:T(8,128)(2,1)}, bf16[704,1024]{1,0:T(8,128)(2,1)S(1)}, u32[]{:S(2)}, u32[]{:S(2)}) collective-permute-start(bf16[704,1024]{1,0:T(8,128)(2,1)} %slice.50), channel_id=1, source_target_pairs={{0,16},{8,24},{16,0},{24,8},{1,17},{9,25},{17,1},{25,9},{2,18},{10... | collective-permute-start | bytes 4325384 | tf_op jit(solution)/shard_map/ppermute | solution.py:24
  77.6 44.5 %collective-permute-start.33 = (bf16[704,1024]{1,0:T(8,128)(2,1)}, bf16[704,1024]{1,0:T(8,128)(2,1)S(1)}, u32[]{:S(2)}, u32[]{:S(2)}) collective-permute-start(bf16[704,1024]{1,0:T(8,128)(2,1)} %slice.50), channel_id=1, source_target_pairs={{0,8},{8,0},{16,24},{24,16},{1,9},{9,1},{17,25},{25,17},{2,10},{10... | collective-permute-start | bytes 4325384 | tf_op jit(solution)/shard_map/ppermute | solution.py:24
  89.3 120.3 %collective-permute-start.30 = (bf16[704,1536]{1,0:T(8,128)(2,1)}, bf16[704,1536]{1,0:T(8,128)(2,1)S(1)}, u32[]{:S(2)}, u32[]{:S(2)}) collective-permute-start(bf16[704,1536]{1,0:T(8,128)(2,1)} %slice.51), channel_id=1, source_target_pairs={{0,16},{8,24},{16,0},{24,8},{1,17},{9,25},{17,1},{25,9},{2,18},{10... | collective-permute-start | bytes 6488072 | tf_op jit(solution)/shard_map/ppermute | solution.py:24
  91.3 94.8 %collective-permute-start.26 = (bf16[704,1024]{1,0:T(8,128)(2,1)}, bf16[704,1024]{1,0:T(8,128)(2,1)S(1)}, u32[]{:S(2)}, u32[]{:S(2)}) collective-permute-start(bf16[704,1024]{1,0:T(8,128)(2,1)} %slice.52), channel_id=1, source_target_pairs={{0,16},{8,24},{16,0},{24,8},{1,17},{9,25},{17,1},{25,9},{2,18},{10... | collective-permute-start | bytes 4325384 | tf_op jit(solution)/shard_map/ppermute | solution.py:24
  110.8 107.2 %collective-permute-start.29 = (bf16[704,1536]{1,0:T(8,128)(2,1)}, bf16[704,1536]{1,0:T(8,128)(2,1)}, u32[]{:S(2)}, u32[]{:S(2)}) collective-permute-start(bf16[704,1536]{1,0:T(8,128)(2,1)} %slice.51), channel_id=1, source_target_pairs={{0,8},{8,0},{16,24},{24,16},{1,9},{9,1},{17,25},{25,17},{2,10},{10... | collective-permute-start | bytes 6488072 | tf_op jit(solution)/shard_map/ppermute | solution.py:24
  122.2 75.8 %collective-permute-start.25 = (bf16[704,1024]{1,0:T(8,128)(2,1)}, bf16[704,1024]{1,0:T(8,128)(2,1)S(1)}, u32[]{:S(2)}, u32[]{:S(2)}) collective-permute-start(bf16[704,1024]{1,0:T(8,128)(2,1)} %slice.52), channel_id=1, source_target_pairs={{0,8},{8,0},{16,24},{24,16},{1,9},{9,1},{17,25},{25,17},{2,10},{10... | collective-permute-start | bytes 4325384 | tf_op jit(solution)/shard_map/ppermute | solution.py:24
  132.1 78.0 %collective-permute-start.17 = (bf16[4,2,72,704]{3,2,1,0:T(8,128)(2,1)}, bf16[4,2,72,704]{3,2,1,0:T(8,128)(2,1)}, u32[]{:S(2)}, u32[]{:S(2)}) collective-permute-start(bf16[4,2,72,704]{3,2,1,0:T(8,128)(2,1)} %collective-permute-done.15.refs_4_), channel_id=1, source_target_pairs={{0,2},{1,3},{2,4},{3,5},{4,6},{5,7},{6,0},{7,1},{8,10},{9,11},{10,... | collective-permute-start | bytes 2433032 | tf_op jit(solution)/shard_map/ppermute | solution.py:212
  186.0 33.5 %collective-permute-start.12 = (bf16[4,2,72,704]{3,2,1,0:T(8,128)(2,1)S(1)}, bf16[4,2,72,704]{3,2,1,0:T(8,128)(2,1)}, u32[]{:S(2)}, u32[]{:S(2)}) collective-permute-start(bf16[4,2,72,704]{3,2,1,0:T(8,128)(2,1)S(1)} %pad_maximum_fusion.refs_0_), channel_id=1, source_target_pairs={{0,1},{1,0},{2,3},{3,2},{4,5},{5,4},{6,7},{7,6},{8,9},{9,8},{10,11... | collective-permute-start | bytes 2433032 | tf_op jit(solution)/shard_map/ppermute | solution.py:24
  218.0 30.7 %collective-permute-start.35 = (bf16[704,512]{1,0:T(8,128)(2,1)}, bf16[704,512]{1,0:T(8,128)(2,1)}, u32[]{:S(2)}, u32[]{:S(2)}) collective-permute-start(bf16[704,512]{1,0:T(8,128)(2,1)} %slice.74), channel_id=1, source_target_pairs={{0,8},{8,0},{16,24},{24,16},{1,9},{9,1},{17,25},{25,17},{2,10},{10... | collective-permute-start | bytes 2162696 | tf_op jit(solution)/shard_map/ppermute | solution.py:24
  219.5 30.7 %collective-permute-start.36 = (bf16[704,512]{1,0:T(8,128)(2,1)}, bf16[704,512]{1,0:T(8,128)(2,1)}, u32[]{:S(2)}, u32[]{:S(2)}) collective-permute-start(bf16[704,512]{1,0:T(8,128)(2,1)} %slice.75), channel_id=1, source_target_pairs={{0,16},{8,24},{16,0},{24,8},{1,17},{9,25},{17,1},{25,9},{2,18},{10... | collective-permute-start | bytes 2162696 | tf_op jit(solution)/shard_map/ppermute | solution.py:24
  226.1 67.6 %collective-permute-start.27 = (bf16[704,512]{1,0:T(8,128)(2,1)}, bf16[704,512]{1,0:T(8,128)(2,1)}, u32[]{:S(2)}, u32[]{:S(2)}) collective-permute-start(bf16[704,512]{1,0:T(8,128)(2,1)} %slice.70), channel_id=1, source_target_pairs={{0,8},{8,0},{16,24},{24,16},{1,9},{9,1},{17,25},{25,17},{2,10},{10... | collective-permute-start | bytes 2162696 | tf_op jit(solution)/shard_map/ppermute | solution.py:24
  226.6 49.3 %collective-permute-start.31 = (bf16[704,768]{1,0:T(8,128)(2,1)}, bf16[704,768]{1,0:T(8,128)(2,1)}, u32[]{:S(2)}, u32[]{:S(2)}) collective-permute-start(bf16[704,768]{1,0:T(8,128)(2,1)} %slice.72), channel_id=1, source_target_pairs={{0,8},{8,0},{16,24},{24,16},{1,9},{9,1},{17,25},{25,17},{2,10},{10... | collective-permute-start | bytes 3244040 | tf_op jit(solution)/shard_map/ppermute | solution.py:24
  228.1 49.4 %collective-permute-start.32 = (bf16[704,768]{1,0:T(8,128)(2,1)}, bf16[704,768]{1,0:T(8,128)(2,1)}, u32[]{:S(2)}, u32[]{:S(2)}) collective-permute-start(bf16[704,768]{1,0:T(8,128)(2,1)} %slice.73), channel_id=1, source_target_pairs={{0,16},{8,24},{16,0},{24,8},{1,17},{9,25},{17,1},{25,9},{2,18},{10... | collective-permute-start | bytes 3244040 | tf_op jit(solution)/shard_map/ppermute | solution.py:24
  248.7 45.5 %collective-permute-start.28 = (bf16[704,512]{1,0:T(8,128)(2,1)}, bf16[704,512]{1,0:T(8,128)(2,1)}, u32[]{:S(2)}, u32[]{:S(2)}) collective-permute-start(bf16[704,512]{1,0:T(8,128)(2,1)} %slice.71), channel_id=1, source_target_pairs={{0,16},{8,24},{16,0},{24,8},{1,17},{9,25},{17,1},{25,9},{2,18},{10... | collective-permute-start | bytes 2162696 | tf_op jit(solution)/shard_map/ppermute | solution.py:24
  250.2 54.6 %collective-permute-start.23 = (bf16[704,256]{1,0:T(8,128)(2,1)}, bf16[704,256]{1,0:T(8,128)(2,1)}, u32[]{:S(2)}, u32[]{:S(2)}) collective-permute-start(bf16[704,256]{1,0:T(8,128)(2,1)} %get-tuple-element.17), channel_id=1, source_target_pairs={{0,8},{8,0},{16,24},{24,16},{1,9},{9,1},{17,25},{25,17},{2,10},{10... | collective-permute-start | bytes 1081352 | tf_op jit(solution)/shard_map/ppermute | solution.py:24
  276.0 28.9 %collective-permute-start.24 = (bf16[704,256]{1,0:T(8,128)(2,1)}, bf16[704,256]{1,0:T(8,128)(2,1)}, u32[]{:S(2)}, u32[]{:S(2)}) collective-permute-start(bf16[704,256]{1,0:T(8,128)(2,1)} %get-tuple-element.15), channel_id=1, source_target_pairs={{0,16},{8,24},{16,0},{24,8},{1,17},{9,25},{17,1},{25,9},{2,18},{10... | collective-permute-start | bytes 1081352 | tf_op jit(solution)/shard_map/ppermute | solution.py:24
  277.5 31.2 %collective-permute-start.20 = (bf16[704,256]{1,0:T(8,128)(2,1)}, bf16[704,256]{1,0:T(8,128)(2,1)}, u32[]{:S(2)}, u32[]{:S(2)}) collective-permute-start(bf16[704,256]{1,0:T(8,128)(2,1)} %get-tuple-element.18), channel_id=1, source_target_pairs={{0,8},{8,0},{16,24},{24,16},{1,9},{9,1},{17,25},{25,17},{2,10},{10... | collective-permute-start | bytes 1081352 | tf_op jit(solution)/shard_map/ppermute | solution.py:24
  (30 other events, 721.4 us)
where the time goes:
time: 313 us
  waiting for transfers between devices  161 us (51%)
  Pallas kernels  60.6 us (19%)
  starting transfers between devices  46.9 us (15%)
  local copies, waits for them, and re-layouts  28.1 us (9%)
  matrix products  10.3 us (3%)
  other arithmetic  5.58 us (2%)
    ppermute x34, waiting for transfers between devices, swap(): return lax.ppermute(x, axis, [(i, i ^ mask) for i in range(size)])  142 us
    pallas_call x6, Pallas kernels, chunk_matmul(): pl.pallas_call(functools.partial(matmul_kernel, terms, row_block(rows), t...  52.1 us
    ppermute x34, starting transfers between devices, swap(): return lax.ppermute(x, axis, [(i, i ^ mask) for i in range(size)])  39.6 us
    slice x8, local copies, waits for them, and re-layouts, on_device(): source = lax.slice_in_dim(source, at, at + half, axis=1)  11.3 us
    all_to_all x1, waiting for transfers between devices, on_device(): lax.all_to_all(grad.reshape(n_tensor, share, tokens), 'tensor', split_axi...  10.3 us
    dot_general x1, matrix products, on_device(): jnp.einsum('etf,esf->ets', acts, acts, preferred_element_type=F32)  9.58 us
    pallas_call x1, Pallas kernels, prepare(): pl.pallas_call(functools.partial(prepare_kernel, n), grid_spec=pltpu.Pref...  8.54 us
    ppermute x3, waiting for transfers between devices, on_device(): piece = lax.ppermute(piece, 'tensor', ring)  8.43 us
  transfers between devices with their start and end apart: 38, of which 17 were waited for; matrix products, arithmetic and copies ran while one was open for 8% of the time, Pallas kernels for 18%

commit v1 on v0

--- a/solution.py
+++ b/solution.py
@@ -11,7 +11,7 @@
 
 BF16, F32 = jnp.bfloat16, jnp.float32
 CLIP_DIVISOR = 80.0
-VMEM_LIMIT = 57 << 20
+VMEM_LIMIT = 51 << 20
 NEAR_SHARES = (2, 3, 2, 2)
 CHUNK_SHARES = (2, 3, 2, 1, 1)
 
@@ -67,7 +67,7 @@
         multiply(0)
 
 
-def chunk_matmul(grads, acts, out, start, width, adds, out_shape):
+def chunk_matmul(grads, acts, out, start, width, adds, out_shape, to=None):
     _, rows, tokens = grads.shape
     tile = math.gcd(width // 2, 256)
     tiles = width // 2 // tile
@@ -85,7 +85,8 @@
             args.append(array)
             specs.append(pl.BlockSpec((tokens, tile), index))
         terms.append((s, len(maps)))
-    window = pl.BlockSpec((rows, tile), lambda j: (0, start // tile + j))
+    first = (start if to is None else to) // tile
+    window = pl.BlockSpec((rows, tile), lambda j: (0, first + j))
     aliases = {}
     if out is not None:
         specs.append(window if adds else pl.BlockSpec(memory_space=pl.ANY))
@@ -104,8 +105,40 @@
             bytes_accessed=2 * len(terms) * tokens * width + 4 * rows * width * (1 + adds),
             transcendentals=0,
         ),
-        name="chunk_matmul",
     )(*args)
+
+
+def finish_kernel(terms, block, *refs):
+    grad_ref, known_ref, out_ref, act_refs = refs[0], refs[1], refs[-1], refs[2:]
+    here = pl.ds(pl.multiple_of(pl.program_id(0) * block, block), block)
+    half = out_ref.shape[1] // 2
+    for side in (0, 1):
+        columns = pl.ds(side * half, half)
+        total = known_ref[here, columns]
+        for k, s in enumerate(terms):
+            total += jnp.dot(grad_ref[s, here, :], act_refs[2 * k + side][...], preferred_element_type=F32)
+        out_ref[:, columns] = total
+
+
+def finish_chunk(grads, known, acts, out, start, width):
+    _, rows, tokens = grads.shape
+    block = rows // 2
+    args = [grads, known] + [half for halves in acts.values() for half in halves]
+    args = [pltpu.with_memory_space_constraint(a, pltpu.VMEM) for a in args]
+    specs = [pl.BlockSpec(memory_space=pltpu.VMEM)] * len(args)
+    return pl.pallas_call(
+        functools.partial(finish_kernel, tuple(acts), block),
+        grid=(rows // block,),
+        in_specs=specs + [pl.BlockSpec(memory_space=pl.ANY)],
+        out_specs=pl.BlockSpec((block, width), lambda i: (i, start // width)),
+        out_shape=jax.ShapeDtypeStruct(out.shape, F32),
+        input_output_aliases={len(args): 0},
+        compiler_params=pltpu.CompilerParams(vmem_limit_bytes=VMEM_LIMIT),
+        cost_estimate=pl.CostEstimate(
+            flops=2 * rows * width * len(acts) * tokens, bytes_accessed=4 * rows * width, transcendentals=0
+        ),
+        name="finish",
+    )(*args, out)
 
 
 def prepare_kernel(n, where_ref, scale_ref, *refs):
@@ -227,9 +260,10 @@
     ahead = [c for c, (start, _) in enumerate(chunks) if start >= spans[-1][0]] if len(spans) > 1 else []
     ahead = ahead if n_dp > 2 else []
     out = None
-    if ahead:
-        first = chunks[ahead[0]][0]
-        out = chunk_matmul(scaled, own_or_near(first), out, first, columns - first, False, out_shape)
+    known_sums = {}
+    for c in ahead:
+        start, width = chunks[c]
+        known_sums[c] = chunk_matmul(scaled, own_or_near(start), None, start, width, False, (out_shape[0], width), 0)
     for c, (start, width) in enumerate(chunks):
         half = width // 2
         known = own_or_near(start)
@@ -248,9 +282,10 @@
                     source = lax.slice_in_dim(source, at, at + half, axis=1)
                 halves_of[mask, side] = (swap(source, "dp", n_dp, bit), 0)
             acts[mask] = (halves_of[mask, 0][0], halves_of[mask, 1][0])
-        if c not in ahead:
-            acts = {**known, **acts}
-        out = chunk_matmul(scaled, acts, out, start, width, c in ahead, out_shape)
+        if c in ahead:
+            out = finish_chunk(scaled, known_sums[c], acts, out, start, width)
+        else:
+            out = chunk_matmul(scaled, {**known, **acts}, out, start, width, False, out_shape)
     return out
 
 

time: 313 us -> 329 us (1.051)
  waiting for transfers between devices: 161 us -> 184 us
  starting transfers between devices: 46.9 us -> 39.5 us
  local copies, waits for them, and re-layouts: 28.1 us -> 34.6 us
  other arithmetic: 5.58 us -> 1.91 us
    ppermute x3, waiting for transfers between devices: 8.43 us -> 33.5 us  [on_device(): piece = lax.ppermute(piece, 'tensor', ring)]
    all_to_all x1, waiting for transfers between devices: 10.3 us -> 0.01 us  [on_device(): lax.all_to_all(grad.reshape(n_tensor, share, tokens), 'tensor', split_axi...]
    ppermute x34, waiting for transfers between devices: 142 us -> 150 us  [swap(): return lax.ppermute(x, axis, [(i, i ^ mask) for i in range(size)])]
    ppermute x34, starting transfers between devices: 39.6 us -> 32.6 us  [swap(): return lax.ppermute(x, axis, [(i, i ^ mask) for i in range(size)])]
    pallas_call x6 -> x5, Pallas kernels: 52.1 us -> 46.8 us  [chunk_matmul(): pl.pallas_call(functools.partial(matmul_kernel, terms, row_block(rows), t...]
    pallas_call x0 -> x2, Pallas kernels: none -> 4.55 us  [finish_chunk(): pl.pallas_call(functools.partial(finish_kernel, tuple(acts), block), grid...]
    unnamed x32 -> x56, local copies, waits for them, and re-layouts: 3.07 us -> 7.48 us
  transfers between devices with their start and end apart: 38 -> 38, of which waited for: 17 -> 15; matrix products, arithmetic and copies ran while one was open for 8% -> 8% of each run, Pallas kernels for 18% -> 17%
where the time goes in v1:
time: 329 us
  waiting for transfers between devices  184 us (56%)
  Pallas kernels  59 us (18%)
  starting transfers between devices  39.5 us (12%)
  local copies, waits for them, and re-layouts  34.6 us (11%)
  matrix products  9.33 us (3%)
    ppermute x34, waiting for transfers between devices, swap(): return lax.ppermute(x, axis, [(i, i ^ mask) for i in range(size)])  150 us
    pallas_call x5, Pallas kernels, chunk_matmul(): pl.pallas_call(functools.partial(matmul_kernel, terms, row_block(rows), t...  46.8 us
    ppermute x3, waiting for transfers between devices, on_device(): piece = lax.ppermute(piece, 'tensor', ring)  33.5 us
    ppermute x34, starting transfers between devices, swap(): return lax.ppermute(x, axis, [(i, i ^ mask) for i in range(size)])  32.6 us
    slice x8, local copies, waits for them, and re-layouts, on_device(): source = lax.slice_in_dim(source, at, at + half, axis=1)  12.9 us
    slice x4, local copies, waits for them, and re-layouts, on_device(): parts.append(lax.slice_in_dim(held, start, start + width, axis=1))  9.81 us
    dot_general x1, matrix products, on_device(): jnp.einsum('etf,esf->ets', acts, acts, preferred_element_type=F32)  8.6 us
    pallas_call x1, Pallas kernels, prepare(): pl.pallas_call(functools.partial(prepare_kernel, n), grid_spec=pltpu.Pref...  7.61 us
  transfers between devices with their start and end apart: 38, of which 15 were waited for; matrix products, arithmetic and copies ran while one was open for 8% of the time, Pallas kernels for 17%

profile of v1, /device:TPU:0, one launch (start us, length us, event | category | flops | bytes accessed | tf_op | source)
XLA Modules:
  0.0 328.5 jit_solution(11872828687222224090)
XLA Ops:
  0.0 2.6 reshape.36
  3.4 8.6 %fusion.9 = f32[2,352,352]{2,1,0:T(8,128)S(1)} fusion(bf16[2,352,4608]{2,1,0:T(8,128)(2,1)} %bitcast.38), kind=kOutput, calls=%fused_computation.27 | convolution fusion | flops 2283798528 | bytes 7479296 | tf_op jit(solution)/shard_map/etf,esf->ets/dot_general | solution.py:213
  12.6 6.0 %all-to-all-start = ((bf16[8,72,704]{2,1,0:T(8,128)(2,1)}), bf16[8,72,704]{2,1,0:T(8,128)(2,1)}, u32[]{:S(2)}, u32[]{:S(2)}) async-start(bf16[8,72,704]{2,1,0:T(8,128)(2,1)} %bitcast.9), calls=%async_computation | async-start | bytes 1769472 | tf_op jit(solution)/shard_map/all_to_all | solution.py:200
  22.1 25.5 %collective-permute-done.4 = f32[2,176,352]{2,1,0:T(8,128)S(1)} collective-permute-done((f32[2,176,352]{2,1,0:T(8,128)S(1)}, f32[2,176,352]{2,1,0:T(8,128)S(1)}, u32[]{:S(2)}, u32[]{:S(2)}) %collective-permute-start.4) | collective-permute-done | bytes 495648 | tf_op jit(solution)/shard_map/ppermute | solution.py:24
  55.8 3.1 slice.51
  58.9 2.7 slice.52
  66.0 56.7 %collective-permute-done = bf16[2,72,704]{2,1,0:T(8,128)(2,1)S(1)} collective-permute-done((bf16[2,72,704]{2,1,0:T(8,128)(2,1)S(1)}, bf16[2,72,704]{2,1,0:T(8,128)(2,1)S(1)}, u32[]{:S(2)}, u32[]{:S(2)}) %collective-permute-start) | collective-permute-done | bytes 202784 | tf_op jit(solution)/shard_map/ppermute | solution.py:24
  124.3 7.0 %collective-permute-done.1 = bf16[2,72,704]{2,1,0:T(8,128)(2,1)S(1)} collective-permute-done((bf16[2,72,704]{2,1,0:T(8,128)(2,1)S(1)}, bf16[2,72,704]{2,1,0:T(8,128)(2,1)S(1)}, u32[]{:S(2)}, u32[]{:S(2)}) %collective-permute-start.1) | collective-permute-done | bytes 202784 | tf_op jit(solution)/shard_map/ppermute | solution.py:24
  132.1 2.8 collective-permute-done.7
  136.3 5.4 %collective-permute-done.2 = bf16[2,72,704]{2,1,0:T(8,128)(2,1)S(1)} collective-permute-done((bf16[2,72,704]{2,1,0:T(8,128)(2,1)S(1)}, bf16[2,72,704]{2,1,0:T(8,128)(2,1)S(1)}, u32[]{:S(2)}, u32[]{:S(2)}) %collective-permute-start.2) | collective-permute-done | bytes 202784 | tf_op jit(solution)/shard_map/ppermute | solution.py:24
  142.2 4.0 %collective-permute-done.8 = f32[2]{0:T(128)S(1)} collective-permute-done((f32[2]{0:T(128)S(1)}, f32[2]{0:T(128)S(1)}, u32[]{:S(2)}, u32[]{:S(2)}) %collective-permute-start.8) | collective-permute-done | bytes 40 | tf_op jit(solution)/shard_map/ppermute | solution.py:24
  152.8 13.9 %collective-permute-done.13.refs_2_ = bf16[4,2,72,704]{3,2,1,0:T(8,128)(2,1)S(1)} collective-permute-done((bf16[4,2,72,704]{3,2,1,0:T(8,128)(2,1)S(1)}, bf16[4,2,72,704]{3,2,1,0:T(8,128)(2,1)S(1)}, u32[]{:S(2)}, u32[]{:S(2)}) %collective-permute-start.13) | collective-permute-done | bytes 811040 | tf_op jit(solution)/shard_map/ppermute | solution.py:245
  166.8 19.6 %collective-permute-done.15.refs_4_ = bf16[4,2,72,704]{3,2,1,0:T(8,128)(2,1)} collective-permute-done((bf16[4,2,72,704]{3,2,1,0:T(8,128)(2,1)S(1)}, bf16[4,2,72,704]{3,2,1,0:T(8,128)(2,1)}, u32[]{:S(2)}, u32[]{:S(2)}) %collective-permute-start.15) | collective-permute-done | bytes 811040 | tf_op jit(solution)/shard_map/ppermute | solution.py:245
  186.5 35.4 %collective-permute-done.20.refs_3_ = bf16[704,1024]{1,0:T(8,128)(2,1)S(1)} collective-permute-done((bf16[704,1024]{1,0:T(8,128)(2,1)S(1)}, bf16[704,1024]{1,0:T(8,128)(2,1)S(1)}, u32[]{:S(2)}, u32[]{:S(2)}) %collective-permute-start.20) | collective-permute-done | bytes 1441824 | tf_op jit(solution)/shard_map/ppermute | solution.py:24
  226.1 3.0 collective-permute-done.10
  230.6 2.9 collective-permute-done.11
  253.1 7.6 %prepare.1 = bf16[4,2,8,72,704]{4,3,2,1,0:T(8,128)(2,1)} custom-call(s32[8]{0:T(128)S(1)} %stack.66.where_ref, f32[4,704]{1,0:T(4,128)S(1)} %reshape.37.scale_ref, bf16[4,2,72,704]{3,2,1,0:T(8,128)(2,1)S(1)} %pad_maximum_fusion.refs_0_, bf16[4,2,72,704]{3,2,1,0:T(8,128)(2,1)S(1)} %collective-permute-done.12.refs_1_, ...), custom_call_target="tpu_custom_call" | custom-call | flops 3244032 | bytes 12976128 | tf_op jit(solution)/shard_map/prepare/pallas_call | solution.py:160
  262.7 3.0 copy-done
  265.7 10.6 %shard_map.39.refs_6_ = f32[1152,4608]{1,0:T(8,128)} custom-call(bf16[4,1152,704]{2,1,0:T(8,128)(2,1)S(1)} %bitcast.31, bf16[704,4608]{1,0:T(8,128)(2,1)} %refs_1_.9, bf16[704,1024]{1,0:T(8,128)(2,1)} %copy-done.10, bf16[704,1024]{1,0:T(8,128)(2,1)} %collective-permute-done.34.refs_3_, bf16[704,512]{1,0:T(8,128)(2,1)} %collective-permute-done.35.refs_4_, ...), custom_call_target="tpu_custom_call" | custom-call | flops 6643777536 | bytes 10485760 | tf_op jit(solution)/shard_map/pallas_call | solution.py:95
  276.3 3.6 %collective-permute-done.31.refs_4_ = bf16[704,768]{1,0:T(8,128)(2,1)} collective-permute-done((bf16[704,768]{1,0:T(8,128)(2,1)}, bf16[704,768]{1,0:T(8,128)(2,1)}, u32[]{:S(2)}, u32[]{:S(2)}) %collective-permute-start.31) | collective-permute-done | bytes 1081376 | tf_op jit(solution)/shard_map/ppermute | solution.py:24
  282.7 14.7 %shard_map.40.refs_6_ = f32[1152,4608]{1,0:T(8,128)} custom-call(bf16[4,1152,704]{2,1,0:T(8,128)(2,1)S(1)} %bitcast.32, bf16[704,4608]{1,0:T(8,128)(2,1)} %refs_1_.9, bf16[704,1536]{1,0:T(8,128)(2,1)} %copy-done.8, bf16[704,1536]{1,0:T(8,128)(2,1)} %copy-done.7, bf16[704,768]{1,0:T(8,128)(2,1)} %collective-permute-done.31.refs_4_, ...), custom_call_target="tpu_custom_call", output_to_operand_aliasing={{}: (6, {})} | custom-call | flops 9965666304 | bytes 15728640 | tf_op jit(solution)/shard_map/pallas_call | solution.py:95
  299.2 10.6 %shard_map.41.refs_4_ = f32[1152,4608]{1,0:T(8,128)} custom-call(bf16[4,1152,704]{2,1,0:T(8,128)(2,1)S(1)} %bitcast.33, bf16[704,4608]{1,0:T(8,128)(2,1)} %refs_1_.9, bf16[704,1024]{1,0:T(8,128)(2,1)} %collective-permute-done.25.refs_2_, bf16[704,1024]{1,0:T(8,128)(2,1)} %collective-permute-done.26.refs_3_, ...), custom_call_target="tpu_custom_call", output_to_operand_aliasing={{}: (6, {})} | custom-call | flops 6643777536 | bytes 10485760 | tf_op jit(solution)/shard_map/pallas_call | solution.py:95
  309.8 5.4 %shard_map.38.refs_1_ = f32[1152,512]{1,0:T(8,128)} custom-call(bf16[4,1152,704]{2,1,0:T(8,128)(2,1)S(1)} %bitcast.34, bf16[704,4608]{1,0:T(8,128)(2,1)} %refs_1_.9, bf16[704,1024]{1,0:T(8,128)(2,1)} %copy-done.3, bf16[704,1024]{1,0:T(8,128)(2,1)} %copy-done.5), custom_call_target="tpu_custom_call" | custom-call | flops 2491416576 | bytes 4521984 | tf_op jit(solution)/shard_map/pallas_call | solution.py:95
  319.1 5.4 %shard_map.37.refs_1_ = f32[1152,512]{1,0:T(8,128)} custom-call(bf16[4,1152,704]{2,1,0:T(8,128)(2,1)S(1)} %bitcast.36, bf16[704,4608]{1,0:T(8,128)(2,1)} %refs_1_.9, bf16[704,1024]{1,0:T(8,128)(2,1)} %copy-done.3, bf16[704,1024]{1,0:T(8,128)(2,1)} %copy-done.5), custom_call_target="tpu_custom_call" | custom-call | flops 2491416576 | bytes 4521984 | tf_op jit(solution)/shard_map/pallas_call | solution.py:95
  (149 shorter events, 68.0 us)
Async XLA Ops:
  12.6 50.0 %all-to-all-start = ((bf16[8,72,704]{2,1,0:T(8,128)(2,1)}), bf16[8,72,704]{2,1,0:T(8,128)(2,1)}, u32[]{:S(2)}, u32[]{:S(2)}) async-start(bf16[8,72,704]{2,1,0:T(8,128)(2,1)} %bitcast.9), calls=%async_computation | async-start | bytes 1769472 | tf_op jit(solution)/shard_map/all_to_all | solution.py:200
  20.0 27.6 %collective-permute-start.4 = (f32[2,176,352]{2,1,0:T(8,128)S(1)}, f32[2,176,352]{2,1,0:T(8,128)S(1)}, u32[]{:S(2)}, u32[]{:S(2)}) collective-permute-start(f32[2,176,352]{2,1,0:T(8,128)S(1)} %constant_dynamic-slice_fusion.1), channel_id=1, source_target_pairs={{0,2},{1,3},{2,0},{3,1},{4,6},{5,7},{6,4},{7,5},{8,10},{9,11},{10,... | collective-permute-start | bytes 1486856 | tf_op jit(solution)/shard_map/ppermute | solution.py:24
  52.8 94.0 %collective-permute-start.34 = (bf16[704,1024]{1,0:T(8,128)(2,1)}, bf16[704,1024]{1,0:T(8,128)(2,1)}, u32[]{:S(2)}, u32[]{:S(2)}) collective-permute-start(bf16[704,1024]{1,0:T(8,128)(2,1)} %slice.50), channel_id=1, source_target_pairs={{0,16},{8,24},{16,0},{24,8},{1,17},{9,25},{17,1},{25,9},{2,18},{10... | collective-permute-start | bytes 4325384 | tf_op jit(solution)/shard_map/ppermute | solution.py:24
  54.3 94.9 %collective-permute-start.33 = (bf16[704,1024]{1,0:T(8,128)(2,1)}, bf16[704,1024]{1,0:T(8,128)(2,1)S(1)}, u32[]{:S(2)}, u32[]{:S(2)}) collective-permute-start(bf16[704,1024]{1,0:T(8,128)(2,1)} %slice.50), channel_id=1, source_target_pairs={{0,8},{8,0},{16,24},{24,16},{1,9},{9,1},{17,25},{25,17},{2,10},{10... | collective-permute-start | bytes 4325384 | tf_op jit(solution)/shard_map/ppermute | solution.py:24
  61.6 89.2 %collective-permute-start.26 = (bf16[704,1024]{1,0:T(8,128)(2,1)}, bf16[704,1024]{1,0:T(8,128)(2,1)}, u32[]{:S(2)}, u32[]{:S(2)}) collective-permute-start(bf16[704,1024]{1,0:T(8,128)(2,1)} %slice.52), channel_id=1, source_target_pairs={{0,16},{8,24},{16,0},{24,8},{1,17},{9,25},{17,1},{25,9},{2,18},{10... | collective-permute-start | bytes 4325384 | tf_op jit(solution)/shard_map/ppermute | solution.py:24
  62.1 89.2 %collective-permute-start.25 = (bf16[704,1024]{1,0:T(8,128)(2,1)}, bf16[704,1024]{1,0:T(8,128)(2,1)}, u32[]{:S(2)}, u32[]{:S(2)}) collective-permute-start(bf16[704,1024]{1,0:T(8,128)(2,1)} %slice.52), channel_id=1, source_target_pairs={{0,8},{8,0},{16,24},{24,16},{1,9},{9,1},{17,25},{25,17},{2,10},{10... | collective-permute-start | bytes 4325384 | tf_op jit(solution)/shard_map/ppermute | solution.py:24
  64.2 58.5 %collective-permute-start = (bf16[2,72,704]{2,1,0:T(8,128)(2,1)S(1)}, bf16[2,72,704]{2,1,0:T(8,128)(2,1)S(1)}, u32[]{:S(2)}, u32[]{:S(2)}) collective-permute-start(bf16[2,72,704]{2,1,0:T(8,128)(2,1)S(1)} %get-tuple-element.22), channel_id=1, source_target_pairs={{0,8},{8,0},{16,24},{24,16},{1,9},{9,1},{17,25},{25,17},{2,10},{10... | collective-permute-start | bytes 608264 | tf_op jit(solution)/shard_map/ppermute | solution.py:24
  146.2 87.3 %collective-permute-start.30 = (bf16[704,1536]{1,0:T(8,128)(2,1)S(1)}, bf16[704,1536]{1,0:T(8,128)(2,1)S(1)}, u32[]{:S(2)}, u32[]{:S(2)}) collective-permute-start(bf16[704,1536]{1,0:T(8,128)(2,1)S(1)} %copy-done.12), channel_id=1, source_target_pairs={{0,16},{8,24},{16,0},{24,8},{1,17},{9,25},{17,1},{25,9},{2,18},{10... | collective-permute-start | bytes 6488072 | tf_op jit(solution)/shard_map/ppermute | solution.py:24
  146.9 19.9 %collective-permute-start.13 = (bf16[4,2,72,704]{3,2,1,0:T(8,128)(2,1)S(1)}, bf16[4,2,72,704]{3,2,1,0:T(8,128)(2,1)S(1)}, u32[]{:S(2)}, u32[]{:S(2)}) collective-permute-start(bf16[4,2,72,704]{3,2,1,0:T(8,128)(2,1)S(1)} %pad_maximum_fusion.refs_0_), channel_id=1, source_target_pairs={{0,2},{1,3},{2,4},{3,5},{4,6},{5,7},{6,0},{7,1},{8,10},{9,11},{10,... | collective-permute-start | bytes 2433032 | tf_op jit(solution)/shard_map/ppermute | solution.py:245
  149.2 37.1 %collective-permute-start.19 = (bf16[704,1024]{1,0:T(8,128)(2,1)S(1)}, bf16[704,1024]{1,0:T(8,128)(2,1)S(1)}, u32[]{:S(2)}, u32[]{:S(2)}) collective-permute-start(bf16[704,1024]{1,0:T(8,128)(2,1)S(1)} %slice.53), channel_id=1, source_target_pairs={{0,8},{8,0},{16,24},{24,16},{1,9},{9,1},{17,25},{25,17},{2,10},{10... | collective-permute-start | bytes 4325384 | tf_op jit(solution)/shard_map/ppermute | solution.py:24
  150.8 86.5 %collective-permute-start.29 = (bf16[704,1536]{1,0:T(8,128)(2,1)S(1)}, bf16[704,1536]{1,0:T(8,128)(2,1)S(1)}, u32[]{:S(2)}, u32[]{:S(2)}) collective-permute-start(bf16[704,1536]{1,0:T(8,128)(2,1)S(1)} %copy-done.12), channel_id=1, source_target_pairs={{0,8},{8,0},{16,24},{24,16},{1,9},{9,1},{17,25},{25,17},{2,10},{10... | collective-permute-start | bytes 6488072 | tf_op jit(solution)/shard_map/ppermute | solution.py:24
  151.3 70.6 %collective-permute-start.20 = (bf16[704,1024]{1,0:T(8,128)(2,1)S(1)}, bf16[704,1024]{1,0:T(8,128)(2,1)S(1)}, u32[]{:S(2)}, u32[]{:S(2)}) collective-permute-start(bf16[704,1024]{1,0:T(8,128)(2,1)S(1)} %slice.53), channel_id=1, source_target_pairs={{0,16},{8,24},{16,0},{24,8},{1,17},{9,25},{17,1},{25,9},{2,18},{10... | collective-permute-start | bytes 4325384 | tf_op jit(solution)/shard_map/ppermute | solution.py:24
  186.4 47.7 %collective-permute-start.17 = (bf16[4,2,72,704]{3,2,1,0:T(8,128)(2,1)}, bf16[4,2,72,704]{3,2,1,0:T(8,128)(2,1)}, u32[]{:S(2)}, u32[]{:S(2)}) collective-permute-start(bf16[4,2,72,704]{3,2,1,0:T(8,128)(2,1)} %collective-permute-done.15.refs_4_), channel_id=1, source_target_pairs={{0,2},{1,3},{2,4},{3,5},{4,6},{5,7},{6,0},{7,1},{8,10},{9,11},{10,... | collective-permute-start | bytes 2433032 | tf_op jit(solution)/shard_map/ppermute | solution.py:245
  186.4 52.5 %collective-permute-start.12 = (bf16[4,2,72,704]{3,2,1,0:T(8,128)(2,1)S(1)}, bf16[4,2,72,704]{3,2,1,0:T(8,128)(2,1)S(1)}, u32[]{:S(2)}, u32[]{:S(2)}) collective-permute-start(bf16[4,2,72,704]{3,2,1,0:T(8,128)(2,1)S(1)} %pad_maximum_fusion.refs_0_), channel_id=1, source_target_pairs={{0,1},{1,0},{2,3},{3,2},{4,5},{5,4},{6,7},{7,6},{8,9},{9,8},{10,11... | collective-permute-start | bytes 2433032 | tf_op jit(solution)/shard_map/ppermute | solution.py:24
  237.3 23.4 %collective-permute-start.35 = (bf16[704,512]{1,0:T(8,128)(2,1)}, bf16[704,512]{1,0:T(8,128)(2,1)}, u32[]{:S(2)}, u32[]{:S(2)}) collective-permute-start(bf16[704,512]{1,0:T(8,128)(2,1)} %slice.74), channel_id=1, source_target_pairs={{0,8},{8,0},{16,24},{24,16},{1,9},{9,1},{17,25},{25,17},{2,10},{10... | collective-permute-start | bytes 2162696 | tf_op jit(solution)/shard_map/ppermute | solution.py:24
  238.9 22.5 %collective-permute-start.36 = (bf16[704,512]{1,0:T(8,128)(2,1)}, bf16[704,512]{1,0:T(8,128)(2,1)}, u32[]{:S(2)}, u32[]{:S(2)}) collective-permute-start(bf16[704,512]{1,0:T(8,128)(2,1)} %slice.75), channel_id=1, source_target_pairs={{0,16},{8,24},{16,0},{24,8},{1,17},{9,25},{17,1},{25,9},{2,18},{10... | collective-permute-start | bytes 2162696 | tf_op jit(solution)/shard_map/ppermute | solution.py:24
  243.1 36.8 %collective-permute-start.31 = (bf16[704,768]{1,0:T(8,128)(2,1)}, bf16[704,768]{1,0:T(8,128)(2,1)}, u32[]{:S(2)}, u32[]{:S(2)}) collective-permute-start(bf16[704,768]{1,0:T(8,128)(2,1)} %slice.72), channel_id=1, source_target_pairs={{0,8},{8,0},{16,24},{24,16},{1,9},{9,1},{17,25},{25,17},{2,10},{10... | collective-permute-start | bytes 3244040 | tf_op jit(solution)/shard_map/ppermute | solution.py:24
  244.4 37.0 %collective-permute-start.32 = (bf16[704,768]{1,0:T(8,128)(2,1)}, bf16[704,768]{1,0:T(8,128)(2,1)}, u32[]{:S(2)}, u32[]{:S(2)}) collective-permute-start(bf16[704,768]{1,0:T(8,128)(2,1)} %slice.73), channel_id=1, source_target_pairs={{0,16},{8,24},{16,0},{24,8},{1,17},{9,25},{17,1},{25,9},{2,18},{10... | collective-permute-start | bytes 3244040 | tf_op jit(solution)/shard_map/ppermute | solution.py:24
  252.4 45.0 %collective-permute-start.27 = (bf16[704,512]{1,0:T(8,128)(2,1)S(1)}, bf16[704,512]{1,0:T(8,128)(2,1)S(1)}, u32[]{:S(2)}, u32[]{:S(2)}) collective-permute-start(bf16[704,512]{1,0:T(8,128)(2,1)S(1)} %copy-done.15), channel_id=1, source_target_pairs={{0,8},{8,0},{16,24},{24,16},{1,9},{9,1},{17,25},{25,17},{2,10},{10... | collective-permute-start | bytes 2162696 | tf_op jit(solution)/shard_map/ppermute | solution.py:24
  260.8 37.5 %collective-permute-start.28 = (bf16[704,512]{1,0:T(8,128)(2,1)S(1)}, bf16[704,512]{1,0:T(8,128)(2,1)S(1)}, u32[]{:S(2)}, u32[]{:S(2)}) collective-permute-start(bf16[704,512]{1,0:T(8,128)(2,1)S(1)} %copy-done.14), channel_id=1, source_target_pairs={{0,16},{8,24},{16,0},{24,8},{1,17},{9,25},{17,1},{25,9},{2,18},{10... | collective-permute-start | bytes 2162696 | tf_op jit(solution)/shard_map/ppermute | solution.py:24
  261.4 53.8 %collective-permute-start.23 = (bf16[704,256]{1,0:T(8,128)(2,1)}, bf16[704,256]{1,0:T(8,128)(2,1)S(1)}, u32[]{:S(2)}, u32[]{:S(2)}) collective-permute-start(bf16[704,256]{1,0:T(8,128)(2,1)} %get-tuple-element.17), channel_id=1, source_target_pairs={{0,8},{8,0},{16,24},{24,16},{1,9},{9,1},{17,25},{25,17},{2,10},{10... | collective-permute-start | bytes 1081352 | tf_op jit(solution)/shard_map/ppermute | solution.py:24
  279.9 35.3 %collective-permute-start.24 = (bf16[704,256]{1,0:T(8,128)(2,1)S(1)}, bf16[704,256]{1,0:T(8,128)(2,1)S(1)}, u32[]{:S(2)}, u32[]{:S(2)}) collective-permute-start(bf16[704,256]{1,0:T(8,128)(2,1)S(1)} %copy-done.20), channel_id=1, source_target_pairs={{0,16},{8,24},{16,0},{24,8},{1,17},{9,25},{17,1},{25,9},{2,18},{10... | collective-permute-start | bytes 1081352 | tf_op jit(solution)/shard_map/ppermute | solution.py:24
  281.4 43.2 %collective-permute-start.21 = (bf16[704,256]{1,0:T(8,128)(2,1)S(1)}, bf16[704,256]{1,0:T(8,128)(2,1)S(1)}, u32[]{:S(2)}, u32[]{:S(2)}) collective-permute-start(bf16[704,256]{1,0:T(8,128)(2,1)S(1)} %copy-done.18), channel_id=1, source_target_pairs={{0,8},{8,0},{16,24},{24,16},{1,9},{9,1},{17,25},{25,17},{2,10},{10... | collective-permute-start | bytes 1081352 | tf_op jit(solution)/shard_map/ppermute | solution.py:24
  297.4 27.2 %collective-permute-start.22 = (bf16[704,256]{1,0:T(8,128)(2,1)S(1)}, bf16[704,256]{1,0:T(8,128)(2,1)S(1)}, u32[]{:S(2)}, u32[]{:S(2)}) collective-permute-start(bf16[704,256]{1,0:T(8,128)(2,1)S(1)} %copy-done.19), channel_id=1, source_target_pairs={{0,16},{8,24},{16,0},{24,8},{1,17},{9,25},{17,1},{25,9},{2,18},{10... | collective-permute-start | bytes 1081352 | tf_op jit(solution)/shard_map/ppermute | solution.py:24
  (42 other events, 614.7 us)

commit v2 on v1

--- a/solution.py
+++ b/solution.py
@@ -108,6 +108,32 @@
     )(*args)
 
 
+def first_columns_kernel(in_ref, out_ref, sems):
+    columns = pl.ds(0, out_ref.shape[1])
+    block = in_ref.shape[0] // sems.shape[0]
+    copies = []
+    for i in range(sems.shape[0]):
+        rows = pl.ds(i * block, block)
+        copies.append(pltpu.make_async_copy(in_ref.at[rows, columns], out_ref.at[rows, :], sems.at[i]))
+    for copy in copies:
+        copy.start()
+    for copy in copies:
+        copy.wait()
+
+
+def first_columns(array, width):
+    rows = array.shape[0]
+    return pl.pallas_call(
+        first_columns_kernel,
+        in_specs=[pl.BlockSpec(memory_space=pltpu.HBM)],
+        out_specs=pl.BlockSpec(memory_space=pltpu.VMEM),
+        out_shape=pltpu.VMEM((rows, width), array.dtype),
+        compiler_params=pltpu.CompilerParams(vmem_limit_bytes=8 << 20),
+        scratch_shapes=[pltpu.SemaphoreType.DMA((4 if rows % 64 == 0 else 1,))],
+        name="first_columns",
+    )(pltpu.with_memory_space_constraint(array, pltpu.HBM))
+
+
 def finish_kernel(terms, block, *refs):
     grad_ref, known_ref, out_ref, act_refs = refs[0], refs[1], refs[-1], refs[2:]
     here = pl.ds(pl.multiple_of(pl.program_id(0) * block, block), block)
@@ -191,7 +217,10 @@
     spans = cut(columns, NEAR_SHARES)
     parts, held = [], hidden_act
     for start, width in spans:
-        parts.append(lax.slice_in_dim(held, start, start + width, axis=1))
+        if start == 0:
+            parts.append(first_columns(held, width))
+        else:
+            parts.append(lax.slice_in_dim(held, start, start + width, axis=1))
         held = after(held, parts[-1])[0]
     blocks = {mask: [swap(parts[0], "dp", n_dp, mask)] for mask in near}
 

time: 329 us -> 329 us (level)
    slice x4 -> x3, local copies, waits for them, and re-layouts: 9.81 us -> 7.16 us  [on_device(): parts.append(lax.slice_in_dim(held, start, start + width, axis=1))]
    unnamed x56 -> x40, local copies, waits for them, and re-layouts: 7.48 us -> 7.3 us
  transfers between devices with their start and end apart: 38 -> 38, of which waited for: 15 -> 15; matrix products, arithmetic and copies ran while one was open for 8% -> 7% of each run, Pallas kernels for 17% -> 18%
where the time goes in v2:
time: 329 us; the launch traced here: 328 us
  waiting for transfers between devices  185 us (56%)
  Pallas kernels  60.3 us (18%)
  starting transfers between devices  39.5 us (12%)
  local copies, waits for them, and re-layouts  31.9 us (10%)
  matrix products  9.33 us (3%)
    ppermute x34, waiting for transfers between devices, swap(): return lax.ppermute(x, axis, [(i, i ^ mask) for i in range(size)])  151 us
    pallas_call x5, Pallas kernels, chunk_matmul(): pl.pallas_call(functools.partial(matmul_kernel, terms, row_block(rows), t...  46.8 us
    ppermute x3, waiting for transfers between devices, on_device(): piece = lax.ppermute(piece, 'tensor', ring)  33.7 us
    ppermute x34, starting transfers between devices, swap(): return lax.ppermute(x, axis, [(i, i ^ mask) for i in range(size)])  32.7 us
    slice x8, local copies, waits for them, and re-layouts, on_device(): source = lax.slice_in_dim(source, at, at + half, axis=1)  13 us
    dot_general x1, matrix products, on_device(): jnp.einsum('etf,esf->ets', acts, acts, preferred_element_type=F32)  8.6 us
    pallas_call x1, Pallas kernels, prepare(): pl.pallas_call(functools.partial(prepare_kernel, n), grid_spec=pltpu.Pref...  7.61 us
    unnamed x40, local copies, waits for them, and re-layouts  7.3 us
  transfers between devices with their start and end apart: 38, of which 15 were waited for; matrix products, arithmetic and copies ran while one was open for 7% of the time, Pallas kernels for 18%

profile of v2, /device:TPU:0, one launch (start us, length us, event | category | flops | bytes accessed | tf_op | source)
XLA Modules:
  0.0 328.2 jit_solution(10937128317059324120)
XLA Ops:
  0.0 2.6 reshape.36
  3.4 8.6 %fusion.9 = f32[2,352,352]{2,1,0:T(8,128)S(1)} fusion(bf16[2,352,4608]{2,1,0:T(8,128)(2,1)} %bitcast.38), kind=kOutput, calls=%fused_computation.27 | convolution fusion | flops 2283798528 | bytes 7479296 | tf_op jit(solution)/shard_map/etf,esf->ets/dot_general | solution.py:242
  12.6 6.0 %all-to-all-start = ((bf16[8,72,704]{2,1,0:T(8,128)(2,1)}), bf16[8,72,704]{2,1,0:T(8,128)(2,1)}, u32[]{:S(2)}, u32[]{:S(2)}) async-start(bf16[8,72,704]{2,1,0:T(8,128)(2,1)} %bitcast.9), calls=%async_computation | async-start | bytes 1769472 | tf_op jit(solution)/shard_map/all_to_all | solution.py:229
  22.1 25.5 %collective-permute-done.4 = f32[2,176,352]{2,1,0:T(8,128)S(1)} collective-permute-done((f32[2,176,352]{2,1,0:T(8,128)S(1)}, f32[2,176,352]{2,1,0:T(8,128)S(1)}, u32[]{:S(2)}, u32[]{:S(2)}) %collective-permute-start.4) | collective-permute-done | bytes 495648 | tf_op jit(solution)/shard_map/ppermute | solution.py:24
  54.7 3.1 slice.47
  57.8 2.6 slice.48
  64.8 56.5 %collective-permute-done = bf16[2,72,704]{2,1,0:T(8,128)(2,1)S(1)} collective-permute-done((bf16[2,72,704]{2,1,0:T(8,128)(2,1)S(1)}, bf16[2,72,704]{2,1,0:T(8,128)(2,1)S(1)}, u32[]{:S(2)}, u32[]{:S(2)}) %collective-permute-start) | collective-permute-done | bytes 202784 | tf_op jit(solution)/shard_map/ppermute | solution.py:24
  123.0 7.0 %collective-permute-done.1 = bf16[2,72,704]{2,1,0:T(8,128)(2,1)S(1)} collective-permute-done((bf16[2,72,704]{2,1,0:T(8,128)(2,1)S(1)}, bf16[2,72,704]{2,1,0:T(8,128)(2,1)S(1)}, u32[]{:S(2)}, u32[]{:S(2)}) %collective-permute-start.1) | collective-permute-done | bytes 202784 | tf_op jit(solution)/shard_map/ppermute | solution.py:24
  130.7 2.8 collective-permute-done.7
  135.0 5.4 %collective-permute-done.2 = bf16[2,72,704]{2,1,0:T(8,128)(2,1)S(1)} collective-permute-done((bf16[2,72,704]{2,1,0:T(8,128)(2,1)S(1)}, bf16[2,72,704]{2,1,0:T(8,128)(2,1)S(1)}, u32[]{:S(2)}, u32[]{:S(2)}) %collective-permute-start.2) | collective-permute-done | bytes 202784 | tf_op jit(solution)/shard_map/ppermute | solution.py:24
  140.8 4.0 %collective-permute-done.8 = f32[2]{0:T(128)S(1)} collective-permute-done((f32[2]{0:T(128)S(1)}, f32[2]{0:T(128)S(1)}, u32[]{:S(2)}, u32[]{:S(2)}) %collective-permute-start.8) | collective-permute-done | bytes 40 | tf_op jit(solution)/shard_map/ppermute | solution.py:24
  151.4 13.9 %collective-permute-done.13.refs_2_ = bf16[4,2,72,704]{3,2,1,0:T(8,128)(2,1)S(1)} collective-permute-done((bf16[4,2,72,704]{3,2,1,0:T(8,128)(2,1)S(1)}, bf16[4,2,72,704]{3,2,1,0:T(8,128)(2,1)S(1)}, u32[]{:S(2)}, u32[]{:S(2)}) %collective-permute-start.13) | collective-permute-done | bytes 811040 | tf_op jit(solution)/shard_map/ppermute | solution.py:274
  165.4 19.8 %collective-permute-done.15.refs_4_ = bf16[4,2,72,704]{3,2,1,0:T(8,128)(2,1)S(1)} collective-permute-done((bf16[4,2,72,704]{3,2,1,0:T(8,128)(2,1)S(1)}, bf16[4,2,72,704]{3,2,1,0:T(8,128)(2,1)S(1)}, u32[]{:S(2)}, u32[]{:S(2)}) %collective-permute-start.15) | collective-permute-done | bytes 811040 | tf_op jit(solution)/shard_map/ppermute | solution.py:274
  185.3 35.2 %collective-permute-done.20.refs_3_ = bf16[704,1024]{1,0:T(8,128)(2,1)S(1)} collective-permute-done((bf16[704,1024]{1,0:T(8,128)(2,1)S(1)}, bf16[704,1024]{1,0:T(8,128)(2,1)S(1)}, u32[]{:S(2)}, u32[]{:S(2)}) %collective-permute-start.20) | collective-permute-done | bytes 1441824 | tf_op jit(solution)/shard_map/ppermute | solution.py:24
  224.7 3.0 collective-permute-done.10
  229.2 2.9 collective-permute-done.11
  251.7 7.6 %prepare.1 = bf16[4,2,8,72,704]{4,3,2,1,0:T(8,128)(2,1)} custom-call(s32[8]{0:T(128)S(1)} %stack.66.where_ref, f32[4,704]{1,0:T(4,128)S(1)} %reshape.37.scale_ref, bf16[4,2,72,704]{3,2,1,0:T(8,128)(2,1)S(1)} %pad_maximum_fusion.refs_0_, bf16[4,2,72,704]{3,2,1,0:T(8,128)(2,1)S(1)} %collective-permute-done.12.refs_1_, ...), custom_call_target="tpu_custom_call" | custom-call | flops 3244032 | bytes 12976128 | tf_op jit(solution)/shard_map/prepare/pallas_call | solution.py:186
  261.2 3.0 copy-done
  264.3 10.6 %shard_map.39.refs_6_ = f32[1152,4608]{1,0:T(8,128)} custom-call(bf16[4,1152,704]{2,1,0:T(8,128)(2,1)S(1)} %bitcast.31, bf16[704,4608]{1,0:T(8,128)(2,1)} %refs_1_.9, bf16[704,1024]{1,0:T(8,128)(2,1)} %collective-permute-done.33.refs_2_, bf16[704,1024]{1,0:T(8,128)(2,1)} %collective-permute-done.34.refs_3_, ...), custom_call_target="tpu_custom_call" | custom-call | flops 6643777536 | bytes 10485760 | tf_op jit(solution)/shard_map/pallas_call | solution.py:95
  274.9 4.7 %collective-permute-done.31.refs_4_ = bf16[704,768]{1,0:T(8,128)(2,1)} collective-permute-done((bf16[704,768]{1,0:T(8,128)(2,1)}, bf16[704,768]{1,0:T(8,128)(2,1)}, u32[]{:S(2)}, u32[]{:S(2)}) %collective-permute-start.31) | collective-permute-done | bytes 1081376 | tf_op jit(solution)/shard_map/ppermute | solution.py:24
  282.4 14.7 %shard_map.40.refs_6_ = f32[1152,4608]{1,0:T(8,128)} custom-call(bf16[4,1152,704]{2,1,0:T(8,128)(2,1)S(1)} %bitcast.32, bf16[704,4608]{1,0:T(8,128)(2,1)} %refs_1_.9, bf16[704,1536]{1,0:T(8,128)(2,1)} %copy-done.8, bf16[704,1536]{1,0:T(8,128)(2,1)} %copy-done.7, bf16[704,768]{1,0:T(8,128)(2,1)} %collective-permute-done.31.refs_4_, ...), custom_call_target="tpu_custom_call", output_to_operand_aliasing={{}: (6, {})} | custom-call | flops 9965666304 | bytes 15728640 | tf_op jit(solution)/shard_map/pallas_call | solution.py:95
  298.9 10.6 %shard_map.41.refs_4_ = f32[1152,4608]{1,0:T(8,128)} custom-call(bf16[4,1152,704]{2,1,0:T(8,128)(2,1)S(1)} %bitcast.33, bf16[704,4608]{1,0:T(8,128)(2,1)} %refs_1_.9, bf16[704,1024]{1,0:T(8,128)(2,1)} %collective-permute-done.25.refs_2_, bf16[704,1024]{1,0:T(8,128)(2,1)} %collective-permute-done.26.refs_3_, ...), custom_call_target="tpu_custom_call", output_to_operand_aliasing={{}: (6, {})} | custom-call | flops 6643777536 | bytes 10485760 | tf_op jit(solution)/shard_map/pallas_call | solution.py:95
  309.5 5.4 %shard_map.38.refs_1_ = f32[1152,512]{1,0:T(8,128)} custom-call(bf16[4,1152,704]{2,1,0:T(8,128)(2,1)S(1)} %bitcast.34, bf16[704,4608]{1,0:T(8,128)(2,1)} %refs_1_.9, bf16[704,1024]{1,0:T(8,128)(2,1)} %copy-done.3, bf16[704,1024]{1,0:T(8,128)(2,1)} %copy-done.5), custom_call_target="tpu_custom_call" | custom-call | flops 2491416576 | bytes 4521984 | tf_op jit(solution)/shard_map/pallas_call | solution.py:95
  318.9 5.4 %shard_map.37.refs_1_ = f32[1152,512]{1,0:T(8,128)} custom-call(bf16[4,1152,704]{2,1,0:T(8,128)(2,1)S(1)} %bitcast.36, bf16[704,4608]{1,0:T(8,128)(2,1)} %refs_1_.9, bf16[704,1024]{1,0:T(8,128)(2,1)} %copy-done.3, bf16[704,1024]{1,0:T(8,128)(2,1)} %copy-done.5), custom_call_target="tpu_custom_call" | custom-call | flops 2491416576 | bytes 4521984 | tf_op jit(solution)/shard_map/pallas_call | solution.py:95
  (133 shorter events, 66.8 us)
Async XLA Ops:
  12.6 48.8 %all-to-all-start = ((bf16[8,72,704]{2,1,0:T(8,128)(2,1)}), bf16[8,72,704]{2,1,0:T(8,128)(2,1)}, u32[]{:S(2)}, u32[]{:S(2)}) async-start(bf16[8,72,704]{2,1,0:T(8,128)(2,1)} %bitcast.9), calls=%async_computation | async-start | bytes 1769472 | tf_op jit(solution)/shard_map/all_to_all | solution.py:229
  20.0 27.6 %collective-permute-start.4 = (f32[2,176,352]{2,1,0:T(8,128)S(1)}, f32[2,176,352]{2,1,0:T(8,128)S(1)}, u32[]{:S(2)}, u32[]{:S(2)}) collective-permute-start(f32[2,176,352]{2,1,0:T(8,128)S(1)} %constant_dynamic-slice_fusion.1), channel_id=1, source_target_pairs={{0,2},{1,3},{2,0},{3,1},{4,6},{5,7},{6,4},{7,5},{8,10},{9,11},{10,... | collective-permute-start | bytes 1486856 | tf_op jit(solution)/shard_map/ppermute | solution.py:24
  51.6 93.9 %collective-permute-start.34 = (bf16[704,1024]{1,0:T(8,128)(2,1)S(1)}, bf16[704,1024]{1,0:T(8,128)(2,1)}, u32[]{:S(2)}, u32[]{:S(2)}) collective-permute-start(bf16[704,1024]{1,0:T(8,128)(2,1)S(1)} %first_columns.1), channel_id=1, source_target_pairs={{0,16},{8,24},{16,0},{24,8},{1,17},{9,25},{17,1},{25,9},{2,18},{10... | collective-permute-start | bytes 4325384 | tf_op jit(solution)/shard_map/ppermute | solution.py:24
  53.2 94.6 %collective-permute-start.33 = (bf16[704,1024]{1,0:T(8,128)(2,1)S(1)}, bf16[704,1024]{1,0:T(8,128)(2,1)}, u32[]{:S(2)}, u32[]{:S(2)}) collective-permute-start(bf16[704,1024]{1,0:T(8,128)(2,1)S(1)} %first_columns.1), channel_id=1, source_target_pairs={{0,8},{8,0},{16,24},{24,16},{1,9},{9,1},{17,25},{25,17},{2,10},{10... | collective-permute-start | bytes 4325384 | tf_op jit(solution)/shard_map/ppermute | solution.py:24
  60.4 89.0 %collective-permute-start.26 = (bf16[704,1024]{1,0:T(8,128)(2,1)}, bf16[704,1024]{1,0:T(8,128)(2,1)}, u32[]{:S(2)}, u32[]{:S(2)}) collective-permute-start(bf16[704,1024]{1,0:T(8,128)(2,1)} %slice.48), channel_id=1, source_target_pairs={{0,16},{8,24},{16,0},{24,8},{1,17},{9,25},{17,1},{25,9},{2,18},{10... | collective-permute-start | bytes 4325384 | tf_op jit(solution)/shard_map/ppermute | solution.py:24
  60.9 89.1 %collective-permute-start.25 = (bf16[704,1024]{1,0:T(8,128)(2,1)}, bf16[704,1024]{1,0:T(8,128)(2,1)}, u32[]{:S(2)}, u32[]{:S(2)}) collective-permute-start(bf16[704,1024]{1,0:T(8,128)(2,1)} %slice.48), channel_id=1, source_target_pairs={{0,8},{8,0},{16,24},{24,16},{1,9},{9,1},{17,25},{25,17},{2,10},{10... | collective-permute-start | bytes 4325384 | tf_op jit(solution)/shard_map/ppermute | solution.py:24
  62.9 58.3 %collective-permute-start = (bf16[2,72,704]{2,1,0:T(8,128)(2,1)S(1)}, bf16[2,72,704]{2,1,0:T(8,128)(2,1)S(1)}, u32[]{:S(2)}, u32[]{:S(2)}) collective-permute-start(bf16[2,72,704]{2,1,0:T(8,128)(2,1)S(1)} %get-tuple-element.22), channel_id=1, source_target_pairs={{0,8},{8,0},{16,24},{24,16},{1,9},{9,1},{17,25},{25,17},{2,10},{10... | collective-permute-start | bytes 608264 | tf_op jit(solution)/shard_map/ppermute | solution.py:24
  144.8 87.3 %collective-permute-start.30 = (bf16[704,1536]{1,0:T(8,128)(2,1)S(1)}, bf16[704,1536]{1,0:T(8,128)(2,1)S(1)}, u32[]{:S(2)}, u32[]{:S(2)}) collective-permute-start(bf16[704,1536]{1,0:T(8,128)(2,1)S(1)} %copy-done.10), channel_id=1, source_target_pairs={{0,16},{8,24},{16,0},{24,8},{1,17},{9,25},{17,1},{25,9},{2,18},{10... | collective-permute-start | bytes 6488072 | tf_op jit(solution)/shard_map/ppermute | solution.py:24
  145.5 19.9 %collective-permute-start.13 = (bf16[4,2,72,704]{3,2,1,0:T(8,128)(2,1)S(1)}, bf16[4,2,72,704]{3,2,1,0:T(8,128)(2,1)S(1)}, u32[]{:S(2)}, u32[]{:S(2)}) collective-permute-start(bf16[4,2,72,704]{3,2,1,0:T(8,128)(2,1)S(1)} %pad_maximum_fusion.refs_0_), channel_id=1, source_target_pairs={{0,2},{1,3},{2,4},{3,5},{4,6},{5,7},{6,0},{7,1},{8,10},{9,11},{10,... | collective-permute-start | bytes 2433032 | tf_op jit(solution)/shard_map/ppermute | solution.py:274
  147.8 37.4 %collective-permute-start.19 = (bf16[704,1024]{1,0:T(8,128)(2,1)S(1)}, bf16[704,1024]{1,0:T(8,128)(2,1)S(1)}, u32[]{:S(2)}, u32[]{:S(2)}) collective-permute-start(bf16[704,1024]{1,0:T(8,128)(2,1)S(1)} %slice.49), channel_id=1, source_target_pairs={{0,8},{8,0},{16,24},{24,16},{1,9},{9,1},{17,25},{25,17},{2,10},{10... | collective-permute-start | bytes 4325384 | tf_op jit(solution)/shard_map/ppermute | solution.py:24
  149.4 87.6 %collective-permute-start.29 = (bf16[704,1536]{1,0:T(8,128)(2,1)S(1)}, bf16[704,1536]{1,0:T(8,128)(2,1)S(1)}, u32[]{:S(2)}, u32[]{:S(2)}) collective-permute-start(bf16[704,1536]{1,0:T(8,128)(2,1)S(1)} %copy-done.10), channel_id=1, source_target_pairs={{0,8},{8,0},{16,24},{24,16},{1,9},{9,1},{17,25},{25,17},{2,10},{10... | collective-permute-start | bytes 6488072 | tf_op jit(solution)/shard_map/ppermute | solution.py:24
  149.9 70.6 %collective-permute-start.20 = (bf16[704,1024]{1,0:T(8,128)(2,1)S(1)}, bf16[704,1024]{1,0:T(8,128)(2,1)S(1)}, u32[]{:S(2)}, u32[]{:S(2)}) collective-permute-start(bf16[704,1024]{1,0:T(8,128)(2,1)S(1)} %slice.49), channel_id=1, source_target_pairs={{0,16},{8,24},{16,0},{24,8},{1,17},{9,25},{17,1},{25,9},{2,18},{10... | collective-permute-start | bytes 4325384 | tf_op jit(solution)/shard_map/ppermute | solution.py:24
  185.2 47.5 %collective-permute-start.17 = (bf16[4,2,72,704]{3,2,1,0:T(8,128)(2,1)S(1)}, bf16[4,2,72,704]{3,2,1,0:T(8,128)(2,1)}, u32[]{:S(2)}, u32[]{:S(2)}) collective-permute-start(bf16[4,2,72,704]{3,2,1,0:T(8,128)(2,1)S(1)} %collective-permute-done.15.refs_4_), channel_id=1, source_target_pairs={{0,2},{1,3},{2,4},{3,5},{4,6},{5,7},{6,0},{7,1},{8,10},{9,11},{10,... | collective-permute-start | bytes 2433032 | tf_op jit(solution)/shard_map/ppermute | solution.py:274
  185.2 53.4 %collective-permute-start.12 = (bf16[4,2,72,704]{3,2,1,0:T(8,128)(2,1)S(1)}, bf16[4,2,72,704]{3,2,1,0:T(8,128)(2,1)S(1)}, u32[]{:S(2)}, u32[]{:S(2)}) collective-permute-start(bf16[4,2,72,704]{3,2,1,0:T(8,128)(2,1)S(1)} %pad_maximum_fusion.refs_0_), channel_id=1, source_target_pairs={{0,1},{1,0},{2,3},{3,2},{4,5},{5,4},{6,7},{7,6},{8,9},{9,8},{10,11... | collective-permute-start | bytes 2433032 | tf_op jit(solution)/shard_map/ppermute | solution.py:24
  237.0 22.3 %collective-permute-start.35 = (bf16[704,512]{1,0:T(8,128)(2,1)}, bf16[704,512]{1,0:T(8,128)(2,1)}, u32[]{:S(2)}, u32[]{:S(2)}) collective-permute-start(bf16[704,512]{1,0:T(8,128)(2,1)} %slice.70), channel_id=1, source_target_pairs={{0,8},{8,0},{16,24},{24,16},{1,9},{9,1},{17,25},{25,17},{2,10},{10... | collective-permute-start | bytes 2162696 | tf_op jit(solution)/shard_map/ppermute | solution.py:24
  238.6 21.3 %collective-permute-start.36 = (bf16[704,512]{1,0:T(8,128)(2,1)}, bf16[704,512]{1,0:T(8,128)(2,1)}, u32[]{:S(2)}, u32[]{:S(2)}) collective-permute-start(bf16[704,512]{1,0:T(8,128)(2,1)} %slice.71), channel_id=1, source_target_pairs={{0,16},{8,24},{16,0},{24,8},{1,17},{9,25},{17,1},{25,9},{2,18},{10... | collective-permute-start | bytes 2162696 | tf_op jit(solution)/shard_map/ppermute | solution.py:24
  242.8 36.8 %collective-permute-start.31 = (bf16[704,768]{1,0:T(8,128)(2,1)}, bf16[704,768]{1,0:T(8,128)(2,1)}, u32[]{:S(2)}, u32[]{:S(2)}) collective-permute-start(bf16[704,768]{1,0:T(8,128)(2,1)} %slice.68), channel_id=1, source_target_pairs={{0,8},{8,0},{16,24},{24,16},{1,9},{9,1},{17,25},{25,17},{2,10},{10... | collective-permute-start | bytes 3244040 | tf_op jit(solution)/shard_map/ppermute | solution.py:24
  244.1 37.0 %collective-permute-start.32 = (bf16[704,768]{1,0:T(8,128)(2,1)}, bf16[704,768]{1,0:T(8,128)(2,1)}, u32[]{:S(2)}, u32[]{:S(2)}) collective-permute-start(bf16[704,768]{1,0:T(8,128)(2,1)} %slice.69), channel_id=1, source_target_pairs={{0,16},{8,24},{16,0},{24,8},{1,17},{9,25},{17,1},{25,9},{2,18},{10... | collective-permute-start | bytes 3244040 | tf_op jit(solution)/shard_map/ppermute | solution.py:24
  250.9 46.2 %collective-permute-start.27 = (bf16[704,512]{1,0:T(8,128)(2,1)}, bf16[704,512]{1,0:T(8,128)(2,1)S(1)}, u32[]{:S(2)}, u32[]{:S(2)}) collective-permute-start(bf16[704,512]{1,0:T(8,128)(2,1)} %slice.66), channel_id=1, source_target_pairs={{0,8},{8,0},{16,24},{24,16},{1,9},{9,1},{17,25},{25,17},{2,10},{10... | collective-permute-start | bytes 2162696 | tf_op jit(solution)/shard_map/ppermute | solution.py:24
  259.3 38.7 %collective-permute-start.28 = (bf16[704,512]{1,0:T(8,128)(2,1)S(1)}, bf16[704,512]{1,0:T(8,128)(2,1)S(1)}, u32[]{:S(2)}, u32[]{:S(2)}) collective-permute-start(bf16[704,512]{1,0:T(8,128)(2,1)S(1)} %slice.67), channel_id=1, source_target_pairs={{0,16},{8,24},{16,0},{24,8},{1,17},{9,25},{17,1},{25,9},{2,18},{10... | collective-permute-start | bytes 2162696 | tf_op jit(solution)/shard_map/ppermute | solution.py:24
  259.9 55.0 %collective-permute-start.23 = (bf16[704,256]{1,0:T(8,128)(2,1)}, bf16[704,256]{1,0:T(8,128)(2,1)S(1)}, u32[]{:S(2)}, u32[]{:S(2)}) collective-permute-start(bf16[704,256]{1,0:T(8,128)(2,1)} %get-tuple-element.17), channel_id=1, source_target_pairs={{0,8},{8,0},{16,24},{24,16},{1,9},{9,1},{17,25},{25,17},{2,10},{10... | collective-permute-start | bytes 1081352 | tf_op jit(solution)/shard_map/ppermute | solution.py:24
  279.6 35.3 %collective-permute-start.24 = (bf16[704,256]{1,0:T(8,128)(2,1)S(1)}, bf16[704,256]{1,0:T(8,128)(2,1)S(1)}, u32[]{:S(2)}, u32[]{:S(2)}) collective-permute-start(bf16[704,256]{1,0:T(8,128)(2,1)S(1)} %copy-done.16), channel_id=1, source_target_pairs={{0,16},{8,24},{16,0},{24,8},{1,17},{9,25},{17,1},{25,9},{2,18},{10... | collective-permute-start | bytes 1081352 | tf_op jit(solution)/shard_map/ppermute | solution.py:24
  281.1 43.2 %collective-permute-start.21 = (bf16[704,256]{1,0:T(8,128)(2,1)S(1)}, bf16[704,256]{1,0:T(8,128)(2,1)S(1)}, u32[]{:S(2)}, u32[]{:S(2)}) collective-permute-start(bf16[704,256]{1,0:T(8,128)(2,1)S(1)} %copy-done.14), channel_id=1, source_target_pairs={{0,8},{8,0},{16,24},{24,16},{1,9},{9,1},{17,25},{25,17},{2,10},{10... | collective-permute-start | bytes 1081352 | tf_op jit(solution)/shard_map/ppermute | solution.py:24
  297.2 27.1 %collective-permute-start.22 = (bf16[704,256]{1,0:T(8,128)(2,1)S(1)}, bf16[704,256]{1,0:T(8,128)(2,1)S(1)}, u32[]{:S(2)}, u32[]{:S(2)}) collective-permute-start(bf16[704,256]{1,0:T(8,128)(2,1)S(1)} %copy-done.15), channel_id=1, source_target_pairs={{0,16},{8,24},{16,0},{24,8},{1,17},{9,25},{17,1},{25,9},{2,18},{10... | collective-permute-start | bytes 1081352 | tf_op jit(solution)/shard_map/ppermute | solution.py:24
  (34 other events, 479.8 us)
